TPU v7x, 32 devices: a whole 2x2x4 slice. The times are simulated.
32 devices in a mesh: gx: 8 (over z, y), gy: 4 (over x, core).
Axes of the slice: x: 2, y: 2, z: 4, core: 2. Of those that a mesh axis runs over, the one named last changes fastest.
Arguments:
- conc: float32 [32, 64, 1024], P('gx', 'gy'), may hold values from -2 to 2
- order: float32 [3, 32, 64, 1024], P(None, 'gx', 'gy'), may hold values from -1.5 to 1.5
Outputs:
- displacement: float32 [3, 32, 64, 1024], P(None, 'gx', 'gy')
- conc_new: float32 [32, 64, 1024], P('gx', 'gy')
- order_new: float32 [3, 32, 64, 1024], P(None, 'gx', 'gy')
All inputs are finite; a program needn't handle non-finite values.
Results may differ from a plain program's by a relative error of at most 0.0001.
Values sent between devices are 32-bit elements; how exact they have to be, the bound alone decides.
A program may use at most 64 MiB of HBM per device.

v0:
```python
import jax
import jax.numpy as jnp
from jax import lax
from jax.sharding import PartitionSpec as P

ITERS = 3


LAME_LAMBDA = 1.0
SHEAR_MODULUS = 1.0
VEGARD_STRAIN = 1.0
TETRA_STRAIN = 2.0
AXIAL_STRAIN = -0.5
COUPLING = 0.5
WELL_DEPTH = 1.0
GRADIENT_CONC = 0.5
GRADIENT_ORDER = 0.5
TIME_STEP = 0.02
MOBILITY = 1.0
RELAXATION = 1.0


def padded_2(block, sides, width, periodic):
    for axis, dim in sides:
        count = lax.axis_size(axis)
        forward = [(i, i + 1) for i in range(count - 1)]
        if periodic:
            forward.append((count - 1, 0))
        backward = [(target, source) for source, target in forward]
        low = lax.ppermute(
            lax.slice_in_dim(block, block.shape[dim] - width, None, axis=dim), axis, forward
        )
        high = lax.ppermute(lax.slice_in_dim(block, 0, width, axis=dim), axis, backward)
        block = jnp.concatenate([low, block, high], axis=dim)
    return block


def coefficient(variant, axis):
    return TETRA_STRAIN if variant == axis else AXIAL_STRAIN


def laplace_rim(extended):
    core = extended[..., 1:-1, 1:-1, :]
    result = -6.0 * core
    result = result + extended[..., 2:, 1:-1, :] + extended[..., :-2, 1:-1, :]
    result = result + extended[..., 1:-1, 2:, :] + extended[..., 1:-1, :-2, :]
    return result + jnp.roll(core, 1, -1) + jnp.roll(core, -1, -1)


def eigen_stress(conc, order):
    misfit = []
    for axis in range(3):
        value = VEGARD_STRAIN * conc
        for variant in range(3):
            value = value + order[variant] * order[variant] * coefficient(variant, axis)
        misfit.append(value)
    trace = misfit[0] + misfit[1] + misfit[2]
    return (misfit, [LAME_LAMBDA * trace + 2.0 * SHEAR_MODULUS * item for item in misfit])


def stencil(padded):
    offsets = [(1, 0, 0), (0, 1, 0), (0, 0, 1)]

    def pick(comp, shift_x, shift_y, shift_z):
        return padded[
            comp,
            1 + shift_x : padded.shape[1] - 1 + shift_x,
            1 + shift_y : padded.shape[2] - 1 + shift_y,
            1 + shift_z : padded.shape[3] - 1 + shift_z,
        ]

    def plus(first, second, sign):
        return tuple((first[k] + sign * second[k] for k in range(3)))

    zero = (0, 0, 0)
    result = []
    for i in range(3):
        center = pick(i, 0, 0, 0)
        laplace = -6.0 * center
        for axis in range(3):
            laplace = laplace + pick(i, *offsets[axis]) + pick(i, *plus(zero, offsets[axis], -1))
        graddiv = pick(i, *offsets[i]) + pick(i, *plus(zero, offsets[i], -1)) - 2.0 * center
        for j in range(3):
            if j != i:
                both = plus(offsets[i], offsets[j], 1)
                cross = plus(offsets[i], offsets[j], -1)
                graddiv = graddiv + 0.25 * (
                    pick(j, *both)
                    - pick(j, *cross)
                    - pick(j, *plus(zero, cross, -1))
                    + pick(j, *plus(zero, both, -1))
                )
        result.append(-SHEAR_MODULUS * laplace - (LAME_LAMBDA + SHEAR_MODULUS) * graddiv)
    return jnp.stack(result)


def normal_strain(padded):
    strain_x = 0.5 * (padded[0, 2:, 1:-1, 1:-1] - padded[0, :-2, 1:-1, 1:-1])
    strain_y = 0.5 * (padded[1, 1:-1, 2:, 1:-1] - padded[1, 1:-1, :-2, 1:-1])
    strain_z = 0.5 * (padded[2, 1:-1, 1:-1, 2:] - padded[2, 1:-1, 1:-1, :-2])
    return [strain_x, strain_y, strain_z]


def operate(field):
    padded = padded_2(field, (("gx", 1), ("gy", 2)), 1, False)
    return (stencil(jnp.pad(padded, ((0, 0), (0, 0), (0, 0), (1, 1)))), padded)


def squares(field):
    return lax.psum(jnp.sum(field * field), ("gx", "gy"))


def per_device(conc, order):
    phase = jnp.concatenate([conc[None], order], axis=0)
    near = padded_2(phase, (("gx", 1), ("gy", 2)), 1, True)
    misfit_near, eigen_near = eigen_stress(near[0], near[1:])
    rhs_x = -0.5 * (eigen_near[0][2:, 1:-1] - eigen_near[0][:-2, 1:-1])
    rhs_y = -0.5 * (eigen_near[1][1:-1, 2:] - eigen_near[1][1:-1, :-2])
    eigen_z = eigen_near[2][1:-1, 1:-1]
    rhs_z = -0.5 * (jnp.roll(eigen_z, -1, -1) - jnp.roll(eigen_z, 1, -1))
    rhs = jnp.stack([rhs_x, rhs_y, rhs_z])
    misfit = [item[1:-1, 1:-1] for item in misfit_near]
    displacement = jnp.zeros_like(rhs)
    residual = rhs
    direction = rhs
    norm_now = squares(residual)
    for step in range(ITERS):
        image, dir_rim = operate(direction)
        alpha = norm_now / lax.psum(jnp.sum(direction * image), ("gx", "gy"))
        displacement = displacement + alpha * direction
        residual = residual - alpha * image
        norm_next = squares(residual)
        direction = residual + norm_next / norm_now * direction
        norm_now = norm_next
    disp_rim = padded_2(displacement, (("gx", 1), ("gy", 2)), 1, False)
    strain = normal_strain(jnp.pad(disp_rim, ((0, 0), (0, 0), (0, 0), (1, 1))))
    strain_trace = strain[0] + strain[1] + strain[2]
    misfit_trace = misfit[0] + misfit[1] + misfit[2]
    stress = [
        LAME_LAMBDA * (strain_trace - misfit_trace) + 2.0 * SHEAR_MODULUS * (strain[a] - misfit[a])
        for a in range(3)
    ]
    total = order[0] * order[0] + order[1] * order[1] + order[2] * order[2]
    potential = conc * conc * conc - conc - COUPLING * total - GRADIENT_CONC * laplace_rim(near[0])
    potential_rim = padded_2(potential, (("gx", 0), ("gy", 1)), 1, True)
    conc_new = conc + TIME_STEP * MOBILITY * laplace_rim(potential_rim)
    order_laplace = laplace_rim(near[1:])
    drives = []
    for variant in range(3):
        elastic = (
            stress[0] * coefficient(variant, 0)
            + stress[1] * coefficient(variant, 1)
            + stress[2] * coefficient(variant, 2)
        )
        drive = (
            (total - WELL_DEPTH - 2.0 * COUPLING * conc) * order[variant]
            - GRADIENT_ORDER * order_laplace[variant]
            - 2.0 * order[variant] * elastic
        )
        drives.append(drive)
    order_new = order - TIME_STEP * RELAXATION * jnp.stack(drives)
    return (displacement, conc_new, order_new)


def solution(mesh):
    return jax.shard_map(
        per_device,
        mesh=mesh,
        in_specs=(P("gx", "gy", None), P(None, "gx", "gy", None)),
        out_specs=(P(None, "gx", "gy", None), P("gx", "gy", None), P(None, "gx", "gy", None)),
        check_vma=False,
    )
```

profile of v0, /device:TPU:0, one launch (start us, length us, event | category | flops | bytes accessed | tf_op | source)
XLA Modules:
  0.0 350.7 jit_solution(715615047021939877)
XLA Ops:
  0.7 1.2 pad_maximum_fusion.52
  1.8 3.0 collective-permute-start
  4.9 3.1 collective-permute-start.1
  8.0 8.1 %collective-permute-done = f32[4,1,16,1024]{3,2,1,0:T(8,128)S(1)} collective-permute-done((f32[4,1,16,1024]{3,2,1,0:T(8,128)S(1)}, f32[4,1,16,1024]{3,2,1,0:T(8,128)S(1)}, u32[]{:S(2)}, u32[]{:S(2)}) %collective-permute-start) | collective-permute-done | bytes 262176 | tf_op jit(solution)/shard_map/ppermute | solution.py:30
  16.1 2.2 collective-permute-done.1
  18.3 1.2 pad_maximum_fusion.56
  19.6 1.7 collective-permute-start.3
  21.3 2.3 collective-permute-done.2
  27.7 2.3 collective-permute-start.5
  30.0 1.3 collective-permute-start.4
  31.3 3.4 collective-permute-done.5
  34.7 4.7 %collective-permute-done.4 = f32[3,1,16,1024]{3,2,1,0:T(8,128)S(1)} collective-permute-done((f32[3,1,16,1024]{3,2,1,0:T(8,128)S(1)}, f32[3,1,16,1024]{3,2,1,0:T(8,128)S(1)}, u32[]{:S(2)}, u32[]{:S(2)}) %collective-permute-start.4) | collective-permute-done | bytes 196640 | tf_op jit(solution)/shard_map/ppermute | solution.py:33
  39.5 2.3 collective-permute-start.7
  41.8 1.3 collective-permute-start.6
  43.1 3.0 collective-permute-done.6
  50.0 43.3 %all-reduce.4 = (f32[]{:T(128)}, f32[]{:T(128)}) all-reduce(f32[]{:T(128)} %get-tuple-element.4, f32[]{:T(128)} %get-tuple-element.3), channel_id=1, replica_groups=mesh['gx'=8,'gy'=4] {'gx','gy'}, use_global_device_ids=true, to_apply=%region_1.2 | all-reduce | flops 2 | bytes 16 | tf_op jit(solution)/shard_map/psum | solution.py:110
  95.5 41.4 %psum.44 = f32[]{:T(128)} all-reduce(f32[]{:T(128)} %get-tuple-element.15), channel_id=1, replica_groups=mesh['gx'=8,'gy'=4] {'gx','gy'}, use_global_device_ids=true, to_apply=%region_5.6 | all-reduce | flops 1 | bytes 8 | tf_op jit(solution)/shard_map/psum | solution.py:110
  138.4 4.4 %collective-permute-start.9 = (f32[3,1,16,1024]{3,2,1,0:T(8,128)S(1)}, f32[3,1,16,1024]{3,2,1,0:T(8,128)S(1)}, u32[]{:S(2)}, u32[]{:S(2)}) collective-permute-start(f32[3,1,16,1024]{3,2,1,0:T(8,128)S(1)} %get-tuple-element.51), channel_id=1, source_target_pairs={{0,4},{4,8},{8,12},{12,16},{16,20},{20,24},{24,28},{1,5},{5,9},{9,... | collective-permute-start | bytes 589832 | tf_op jit(solution)/shard_map/ppermute | solution.py:30
  142.8 1.3 collective-permute-start.8
  144.1 6.1 %collective-permute-done.9 = f32[3,1,16,1024]{3,2,1,0:T(8,128)S(1)} collective-permute-done((f32[3,1,16,1024]{3,2,1,0:T(8,128)S(1)}, f32[3,1,16,1024]{3,2,1,0:T(8,128)S(1)}, u32[]{:S(2)}, u32[]{:S(2)}) %collective-permute-start.9) | collective-permute-done | bytes 196640 | tf_op jit(solution)/shard_map/ppermute | solution.py:30
  150.5 1.3 collective-permute-start.11
  151.8 1.3 collective-permute-start.10
  153.1 2.7 collective-permute-done.10
  159.7 42.6 %psum.45 = f32[]{:T(128)} all-reduce(f32[]{:T(128)} %multiply_reduce_fusion.1), channel_id=1, replica_groups=mesh['gx'=8,'gy'=4] {'gx','gy'}, use_global_device_ids=true, to_apply=%region_7.8 | all-reduce | flops 1 | bytes 8 | tf_op jit(solution)/shard_map/psum | solution.py:129
  204.5 1.4 fusion.135
  205.9 40.7 %psum.46 = f32[]{:T(128)} all-reduce(f32[]{:T(128)} %multiply_reduce_fusion), channel_id=1, replica_groups=mesh['gx'=8,'gy'=4] {'gx','gy'}, use_global_device_ids=true, to_apply=%region_9.10 | all-reduce | flops 1 | bytes 8 | tf_op jit(solution)/shard_map/psum | solution.py:110
  247.8 1.3 multiply_add_fusion.1
  249.3 4.5 %collective-permute-start.13 = (f32[3,1,16,1024]{3,2,1,0:T(8,128)S(1)}, f32[3,1,16,1024]{3,2,1,0:T(8,128)S(1)}, u32[]{:S(2)}, u32[]{:S(2)}) collective-permute-start(f32[3,1,16,1024]{3,2,1,0:T(8,128)S(1)} %get-tuple-element.49), channel_id=1, source_target_pairs={{0,4},{4,8},{8,12},{12,16},{16,20},{20,24},{24,28},{1,5},{5,9},{9,... | collective-permute-start | bytes 589832 | tf_op jit(solution)/shard_map/ppermute | solution.py:30
  253.8 1.3 collective-permute-start.12
  255.2 6.0 %collective-permute-done.13 = f32[3,1,16,1024]{3,2,1,0:T(8,128)S(1)} collective-permute-done((f32[3,1,16,1024]{3,2,1,0:T(8,128)S(1)}, f32[3,1,16,1024]{3,2,1,0:T(8,128)S(1)}, u32[]{:S(2)}, u32[]{:S(2)}) %collective-permute-start.13) | collective-permute-done | bytes 196640 | tf_op jit(solution)/shard_map/ppermute | solution.py:30
  261.4 1.3 collective-permute-start.15
  262.7 1.3 collective-permute-start.14
  264.1 1.3 fusion.3
  265.4 1.3 collective-permute-done.14
  270.4 1.9 slice_bitcast_fusion
  272.4 42.5 %psum.47 = f32[]{:T(128)} all-reduce(f32[]{:T(128)} %fusion.7), channel_id=1, replica_groups=mesh['gx'=8,'gy'=4] {'gx','gy'}, use_global_device_ids=true, to_apply=%region_11.12 | all-reduce | flops 1 | bytes 8 | tf_op jit(solution)/shard_map/psum | solution.py:129
  316.4 4.4 %collective-permute-start.21 = (f32[3,1,16,1024]{3,2,1,0:T(8,128)S(1)}, f32[3,1,16,1024]{3,2,1,0:T(8,128)S(1)}, u32[]{:S(2)}, u32[]{:S(2)}) collective-permute-start(f32[3,1,16,1024]{3,2,1,0:T(8,128)S(1)} %get-tuple-element.43), channel_id=1, source_target_pairs={{0,4},{4,8},{8,12},{12,16},{16,20},{20,24},{24,28},{1,5},{5,9},{9,... | collective-permute-start | bytes 589832 | tf_op jit(solution)/shard_map/ppermute | solution.py:30
  320.8 1.3 collective-permute-start.20
  322.2 6.0 %collective-permute-done.21 = f32[3,1,16,1024]{3,2,1,0:T(8,128)S(1)} collective-permute-done((f32[3,1,16,1024]{3,2,1,0:T(8,128)S(1)}, f32[3,1,16,1024]{3,2,1,0:T(8,128)S(1)}, u32[]{:S(2)}, u32[]{:S(2)}) %collective-permute-start.21) | collective-permute-done | bytes 196640 | tf_op jit(solution)/shard_map/ppermute | solution.py:30
  328.5 1.4 collective-permute-start.23
  329.9 1.3 collective-permute-start.22
  331.3 3.3 collective-permute-done.22
  334.7 1.0 select_maximum_fusion
  337.8 2.3 collective-permute-start.17
  340.2 2.4 collective-permute-start.16
  343.8 1.2 collective-permute-done.17
  345.4 1.9 collective-permute-start.19
  347.9 1.9 collective-permute-done.19
  (108 shorter events, 24.1 us)
Async XLA Ops:
  0.6 17.6 %copy-start = (f32[3,4,16,1024]{3,2,1,0:T(8,128)S(1)}, f32[3,4,16,1024]{3,2,1,0:T(8,128)}, u32[]{:S(2)}) copy-start(f32[3,4,16,1024]{3,2,1,0:T(8,128)} %param.3) | copy-start | bytes 2359300
  0.6 23.7 %copy-start.2 = (f32[4,16,1024]{2,1,0:T(8,128)S(1)}, f32[4,16,1024]{2,1,0:T(8,128)}, u32[]{:S(2)}) copy-start(f32[4,16,1024]{2,1,0:T(8,128)} %param.2) | copy-start | bytes 786436
  1.8 14.2 %collective-permute-start = (f32[4,1,16,1024]{3,2,1,0:T(8,128)S(1)}, f32[4,1,16,1024]{3,2,1,0:T(8,128)S(1)}, u32[]{:S(2)}, u32[]{:S(2)}) collective-permute-start(f32[4,1,16,1024]{3,2,1,0:T(8,128)S(1)} %get-tuple-element.41), channel_id=1, source_target_pairs={{0,4},{4,8},{8,12},{12,16},{16,20},{20,24},{24,28},{28,0},{1,5},{5... | collective-permute-start | bytes 786440 | tf_op jit(solution)/shard_map/ppermute | solution.py:30
  4.9 13.4 %collective-permute-start.1 = (f32[4,1,16,1024]{3,2,1,0:T(8,128)S(1)}, f32[4,1,16,1024]{3,2,1,0:T(8,128)S(1)}, u32[]{:S(2)}, u32[]{:S(2)}) collective-permute-start(f32[4,1,16,1024]{3,2,1,0:T(8,128)S(1)} %get-tuple-element.42), channel_id=1, source_target_pairs={{4,0},{8,4},{12,8},{16,12},{20,16},{24,20},{28,24},{0,28},{5,1},{9... | collective-permute-start | bytes 786440 | tf_op jit(solution)/shard_map/ppermute | solution.py:33
  16.1 7.6 %copy-start.17 = (f32[4,1,16,1024]{3,2,1,0:T(8,128)}, f32[4,1,16,1024]{3,2,1,0:T(8,128)S(1)}, u32[]{:S(2)}) copy-start(f32[4,1,16,1024]{3,2,1,0:T(8,128)S(1)} %collective-permute-done) | copy-start | bytes 786436
  18.3 5.4 %copy-start.19 = (f32[4,1,16,1024]{3,2,1,0:T(8,128)}, f32[4,1,16,1024]{3,2,1,0:T(8,128)S(1)}, u32[]{:S(2)}) copy-start(f32[4,1,16,1024]{3,2,1,0:T(8,128)S(1)} %collective-permute-done.1) | copy-start | bytes 786436
  19.5 4.1 %collective-permute-start.2 = (f32[4,6,1,1024]{3,2,1,0:T(1,128)S(1)}, f32[4,6,1,1024]{3,2,1,0:T(1,128)S(1)}, u32[]{:S(2)}, u32[]{:S(2)}) collective-permute-start(f32[4,6,1,1024]{3,2,1,0:T(1,128)S(1)} %get-tuple-element.25), channel_id=1, source_target_pairs={{0,1},{1,2},{2,3},{3,0},{4,5},{5,6},{6,7},{7,4},{8,9},{9,10},{10,1... | collective-permute-start | bytes 294920 | tf_op jit(solution)/shard_map/ppermute | solution.py:30
  19.6 4.1 %collective-permute-start.3 = (f32[4,6,1,1024]{3,2,1,0:T(1,128)S(1)}, f32[4,6,1,1024]{3,2,1,0:T(1,128)S(1)}, u32[]{:S(2)}, u32[]{:S(2)}) collective-permute-start(f32[4,6,1,1024]{3,2,1,0:T(1,128)S(1)} %get-tuple-element.26), channel_id=1, source_target_pairs={{1,0},{2,1},{3,2},{0,3},{5,4},{6,5},{7,6},{4,7},{9,8},{10,9},{11,1... | collective-permute-start | bytes 294920 | tf_op jit(solution)/shard_map/ppermute | solution.py:33
  23.7 0.7 copy-start.21
  24.7 1.4 copy-start.3
  26.1 0.8 copy-start.5
  26.1 1.0 copy-start.7
  26.1 1.2 copy-start.9
  27.7 7.0 %collective-permute-start.5 = (f32[3,1,16,1024]{3,2,1,0:T(8,128)S(1)}, f32[3,1,16,1024]{3,2,1,0:T(8,128)S(1)}, u32[]{:S(2)}, u32[]{:S(2)}) collective-permute-start(f32[3,1,16,1024]{3,2,1,0:T(8,128)S(1)} %get-tuple-element.53), channel_id=1, source_target_pairs={{0,4},{4,8},{8,12},{12,16},{16,20},{20,24},{24,28},{1,5},{5,9},{9,... | collective-permute-start | bytes 589832 | tf_op jit(solution)/shard_map/ppermute | solution.py:30
  30.0 9.4 %collective-permute-start.4 = (f32[3,1,16,1024]{3,2,1,0:T(8,128)S(1)}, f32[3,1,16,1024]{3,2,1,0:T(8,128)S(1)}, u32[]{:S(2)}, u32[]{:S(2)}) collective-permute-start(f32[3,1,16,1024]{3,2,1,0:T(8,128)S(1)} %get-tuple-element.54), channel_id=1, source_target_pairs={{4,0},{8,4},{12,8},{16,12},{20,16},{24,20},{28,24},{5,1},{9,5},{13... | collective-permute-start | bytes 589832 | tf_op jit(solution)/shard_map/ppermute | solution.py:33
  39.5 3.6 %collective-permute-start.7 = (f32[3,6,1,1024]{3,2,1,0:T(1,128)S(1)}, f32[3,6,1,1024]{3,2,1,0:T(1,128)S(1)}, u32[]{:S(2)}, u32[]{:S(2)}) collective-permute-start(f32[3,6,1,1024]{3,2,1,0:T(1,128)S(1)} %get-tuple-element.39), channel_id=1, source_target_pairs={{0,1},{1,2},{2,3},{4,5},{5,6},{6,7},{8,9},{9,10},{10,11},{12,13},{... | collective-permute-start | bytes 221192 | tf_op jit(solution)/shard_map/ppermute | solution.py:30
  41.8 4.3 %collective-permute-start.6 = (f32[3,6,1,1024]{3,2,1,0:T(1,128)S(1)}, f32[3,6,1,1024]{3,2,1,0:T(1,128)S(1)}, u32[]{:S(2)}, u32[]{:S(2)}) collective-permute-start(f32[3,6,1,1024]{3,2,1,0:T(1,128)S(1)} %get-tuple-element.40), channel_id=1, source_target_pairs={{1,0},{2,1},{3,2},{5,4},{6,5},{7,6},{9,8},{10,9},{11,10},{13,12},{... | collective-permute-start | bytes 221192 | tf_op jit(solution)/shard_map/ppermute | solution.py:33
  138.4 11.8 %collective-permute-start.9 = (f32[3,1,16,1024]{3,2,1,0:T(8,128)S(1)}, f32[3,1,16,1024]{3,2,1,0:T(8,128)S(1)}, u32[]{:S(2)}, u32[]{:S(2)}) collective-permute-start(f32[3,1,16,1024]{3,2,1,0:T(8,128)S(1)} %get-tuple-element.51), channel_id=1, source_target_pairs={{0,4},{4,8},{8,12},{12,16},{16,20},{20,24},{24,28},{1,5},{5,9},{9,... | collective-permute-start | bytes 589832 | tf_op jit(solution)/shard_map/ppermute | solution.py:30
  142.8 7.6 %collective-permute-start.8 = (f32[3,1,16,1024]{3,2,1,0:T(8,128)S(1)}, f32[3,1,16,1024]{3,2,1,0:T(8,128)S(1)}, u32[]{:S(2)}, u32[]{:S(2)}) collective-permute-start(f32[3,1,16,1024]{3,2,1,0:T(8,128)S(1)} %get-tuple-element.52), channel_id=1, source_target_pairs={{4,0},{8,4},{12,8},{16,12},{20,16},{24,20},{28,24},{5,1},{9,5},{13... | collective-permute-start | bytes 589832 | tf_op jit(solution)/shard_map/ppermute | solution.py:33
  150.5 2.6 collective-permute-start.11
  151.8 4.0 %collective-permute-start.10 = (f32[3,6,1,1024]{3,2,1,0:T(1,128)S(1)}, f32[3,6,1,1024]{3,2,1,0:T(1,128)S(1)}, u32[]{:S(2)}, u32[]{:S(2)}) collective-permute-start(f32[3,6,1,1024]{3,2,1,0:T(1,128)S(1)} %get-tuple-element.36), channel_id=1, source_target_pairs={{1,0},{2,1},{3,2},{5,4},{6,5},{7,6},{9,8},{10,9},{11,10},{13,12},{... | collective-permute-start | bytes 221192 | tf_op jit(solution)/shard_map/ppermute | solution.py:33
  157.7 45.9 %copy-start.11 = (f32[1,4,16,1024]{3,2,1,0:T(8,128)}, f32[1,4,16,1024]{3,2,1,0:T(8,128)S(1)}, u32[]{:S(2)}) copy-start(f32[1,4,16,1024]{3,2,1,0:T(8,128)S(1)} %fusion.93) | copy-start | bytes 786436
  158.2 45.5 %copy-start.12 = (f32[1,4,16,1024]{3,2,1,0:T(8,128)}, f32[1,4,16,1024]{3,2,1,0:T(8,128)S(1)}, u32[]{:S(2)}) copy-start(f32[1,4,16,1024]{3,2,1,0:T(8,128)S(1)} %fusion.84) | copy-start | bytes 786436
  158.8 47.1 %copy-start.13 = (f32[1,4,16,1024]{3,2,1,0:T(8,128)}, f32[1,4,16,1024]{3,2,1,0:T(8,128)S(1)}, u32[]{:S(2)}) copy-start(f32[1,4,16,1024]{3,2,1,0:T(8,128)S(1)} %fusion.73) | copy-start | bytes 786436
  249.2 14.9 %copy-start.15 = (f32[3,4,16,1023]{3,2,1,0:T(8,128)S(1)}, f32[3,4,16,1023]{3,2,1,0:T(8,128)}, u32[]{:S(2)}) copy-start(f32[3,4,16,1023]{3,2,1,0:T(8,128)} %get-tuple-element.45) | copy-start | bytes 2356996
  249.2 14.9 %copy-start.16 = (f32[3,4,16,1023]{3,2,1,0:T(8,128)S(1)}, f32[3,4,16,1023]{3,2,1,0:T(8,128)}, u32[]{:S(2)}) copy-start(f32[3,4,16,1023]{3,2,1,0:T(8,128)} %get-tuple-element.46) | copy-start | bytes 2356996
  249.2 14.9 %copy-start.18 = (f32[4,1,16,1024]{3,2,1,0:T(8,128)S(1)}, f32[4,1,16,1024]{3,2,1,0:T(8,128)}, u32[]{:S(2)}) copy-start(f32[4,1,16,1024]{3,2,1,0:T(8,128)} %copy-done.17) | copy-start | bytes 786436
  249.2 14.9 %copy-start.20 = (f32[4,1,16,1024]{3,2,1,0:T(8,128)S(1)}, f32[4,1,16,1024]{3,2,1,0:T(8,128)}, u32[]{:S(2)}) copy-start(f32[4,1,16,1024]{3,2,1,0:T(8,128)} %copy-done.19) | copy-start | bytes 786436
  249.2 14.9 %copy-start.22 = (f32[4,6,1,1024]{3,2,1,0:T(1,128)S(1)}, f32[4,6,1,1024]{3,2,1,0:T(1,128)}, u32[]{:S(2)}) copy-start(f32[4,6,1,1024]{3,2,1,0:T(1,128)} %copy-done.21) | copy-start | bytes 294916
  249.3 11.9 %collective-permute-start.13 = (f32[3,1,16,1024]{3,2,1,0:T(8,128)S(1)}, f32[3,1,16,1024]{3,2,1,0:T(8,128)S(1)}, u32[]{:S(2)}, u32[]{:S(2)}) collective-permute-start(f32[3,1,16,1024]{3,2,1,0:T(8,128)S(1)} %get-tuple-element.49), channel_id=1, source_target_pairs={{0,4},{4,8},{8,12},{12,16},{16,20},{20,24},{24,28},{1,5},{5,9},{9,... | collective-permute-start | bytes 589832 | tf_op jit(solution)/shard_map/ppermute | solution.py:30
  253.8 7.6 %collective-permute-start.12 = (f32[3,1,16,1024]{3,2,1,0:T(8,128)S(1)}, f32[3,1,16,1024]{3,2,1,0:T(8,128)S(1)}, u32[]{:S(2)}, u32[]{:S(2)}) collective-permute-start(f32[3,1,16,1024]{3,2,1,0:T(8,128)S(1)} %get-tuple-element.50), channel_id=1, source_target_pairs={{4,0},{8,4},{12,8},{16,12},{20,16},{24,20},{28,24},{5,1},{9,5},{13... | collective-permute-start | bytes 589832 | tf_op jit(solution)/shard_map/ppermute | solution.py:33
  261.4 4.0 %collective-permute-start.15 = (f32[3,6,1,1024]{3,2,1,0:T(1,128)S(1)}, f32[3,6,1,1024]{3,2,1,0:T(1,128)S(1)}, u32[]{:S(2)}, u32[]{:S(2)}) collective-permute-start(f32[3,6,1,1024]{3,2,1,0:T(1,128)S(1)} %get-tuple-element.31), channel_id=1, source_target_pairs={{0,1},{1,2},{2,3},{4,5},{5,6},{6,7},{8,9},{9,10},{10,11},{12,13},{... | collective-permute-start | bytes 221192 | tf_op jit(solution)/shard_map/ppermute | solution.py:30
  262.7 4.0 %collective-permute-start.14 = (f32[3,6,1,1024]{3,2,1,0:T(1,128)S(1)}, f32[3,6,1,1024]{3,2,1,0:T(1,128)S(1)}, u32[]{:S(2)}, u32[]{:S(2)}) collective-permute-start(f32[3,6,1,1024]{3,2,1,0:T(1,128)S(1)} %get-tuple-element.32), channel_id=1, source_target_pairs={{1,0},{2,1},{3,2},{5,4},{6,5},{7,6},{9,8},{10,9},{11,10},{13,12},{... | collective-permute-start | bytes 221192 | tf_op jit(solution)/shard_map/ppermute | solution.py:33
  316.1 6.0 %copy-start.4 = (f32[6,18,1024]{2,1,0:T(8,128)S(1)}, f32[6,18,1024]{2,1,0:T(8,128)}, u32[]{:S(2)}) copy-start(f32[6,18,1024]{2,1,0:T(8,128)} %slice_bitcast_fusion) | copy-start | bytes 1327108
  316.4 19.4 %copy-start.1 = (f32[3,4,16,1024]{3,2,1,0:T(8,128)}, f32[3,4,16,1024]{3,2,1,0:T(8,128)S(1)}, u32[]{:S(2)}) copy-start(f32[3,4,16,1024]{3,2,1,0:T(8,128)S(1)} %multiply_add_fusion) | copy-start | bytes 2359300
  316.4 11.8 %collective-permute-start.21 = (f32[3,1,16,1024]{3,2,1,0:T(8,128)S(1)}, f32[3,1,16,1024]{3,2,1,0:T(8,128)S(1)}, u32[]{:S(2)}, u32[]{:S(2)}) collective-permute-start(f32[3,1,16,1024]{3,2,1,0:T(8,128)S(1)} %get-tuple-element.43), channel_id=1, source_target_pairs={{0,4},{4,8},{8,12},{12,16},{16,20},{20,24},{24,28},{1,5},{5,9},{9,... | collective-permute-start | bytes 589832 | tf_op jit(solution)/shard_map/ppermute | solution.py:30
  320.8 7.6 %collective-permute-start.20 = (f32[3,1,16,1024]{3,2,1,0:T(8,128)S(1)}, f32[3,1,16,1024]{3,2,1,0:T(8,128)S(1)}, u32[]{:S(2)}, u32[]{:S(2)}) collective-permute-start(f32[3,1,16,1024]{3,2,1,0:T(8,128)S(1)} %get-tuple-element.44), channel_id=1, source_target_pairs={{4,0},{8,4},{12,8},{16,12},{20,16},{24,20},{28,24},{5,1},{9,5},{13... | collective-permute-start | bytes 589832 | tf_op jit(solution)/shard_map/ppermute | solution.py:33
  328.5 7.3 %copy-start.6 = (f32[6,18,1024]{2,1,0:T(8,128)S(1)}, f32[6,18,1024]{2,1,0:T(8,128)}, u32[]{:S(2)}) copy-start(f32[6,18,1024]{2,1,0:T(8,128)} %copy-done.5) | copy-start | bytes 1327108
  328.5 7.3 %copy-start.8 = (f32[6,18,1024]{2,1,0:T(8,128)S(1)}, f32[6,18,1024]{2,1,0:T(8,128)}, u32[]{:S(2)}) copy-start(f32[6,18,1024]{2,1,0:T(8,128)} %copy-done.7) | copy-start | bytes 1327108
  328.5 7.3 %copy-start.10 = (f32[6,18,1024]{2,1,0:T(8,128)S(1)}, f32[6,18,1024]{2,1,0:T(8,128)}, u32[]{:S(2)}) copy-start(f32[6,18,1024]{2,1,0:T(8,128)} %copy-done.9) | copy-start | bytes 1327108
  328.5 2.8 collective-permute-start.23
  329.9 4.7 %collective-permute-start.22 = (f32[3,6,1,1024]{3,2,1,0:T(1,128)S(1)}, f32[3,6,1,1024]{3,2,1,0:T(1,128)S(1)}, u32[]{:S(2)}, u32[]{:S(2)}) collective-permute-start(f32[3,6,1,1024]{3,2,1,0:T(1,128)S(1)} %get-tuple-element.28), channel_id=1, source_target_pairs={{1,0},{2,1},{3,2},{5,4},{6,5},{7,6},{9,8},{10,9},{11,10},{13,12},{... | collective-permute-start | bytes 221192 | tf_op jit(solution)/shard_map/ppermute | solution.py:33
  335.8 1.1 copy-start.14
  337.8 7.1 %collective-permute-start.17 = (f32[1,16,1024]{2,1,0:T(8,128)S(1)}, f32[1,16,1024]{2,1,0:T(8,128)S(1)}, u32[]{:S(2)}, u32[]{:S(2)}) collective-permute-start(f32[1,16,1024]{2,1,0:T(8,128)S(1)} %get-tuple-element.70), channel_id=1, source_target_pairs={{0,4},{4,8},{8,12},{12,16},{16,20},{20,24},{24,28},{28,0},{1,5},{5... | collective-permute-start | bytes 196616 | tf_op jit(solution)/shard_map/ppermute | solution.py:30
  340.2 5.1 %collective-permute-start.16 = (f32[1,16,1024]{2,1,0:T(8,128)S(1)}, f32[1,16,1024]{2,1,0:T(8,128)S(1)}, u32[]{:S(2)}, u32[]{:S(2)}) collective-permute-start(f32[1,16,1024]{2,1,0:T(8,128)S(1)} %get-tuple-element.71), channel_id=1, source_target_pairs={{4,0},{8,4},{12,8},{16,12},{20,16},{24,20},{28,24},{0,28},{5,1},{9... | collective-permute-start | bytes 196616 | tf_op jit(solution)/shard_map/ppermute | solution.py:33
  345.3 2.6 collective-permute-start.18
  345.4 4.5 %collective-permute-start.19 = (f32[6,1,1024]{2,1,0:T(1,128)S(1)}, f32[6,1,1024]{2,1,0:T(1,128)S(1)}, u32[]{:S(2)}, u32[]{:S(2)}) collective-permute-start(f32[6,1,1024]{2,1,0:T(1,128)S(1)} %get-tuple-element.65), channel_id=1, source_target_pairs={{0,1},{1,2},{2,3},{3,0},{4,5},{5,6},{6,7},{7,4},{8,9},{9,10},{10,1... | collective-permute-start | bytes 73736 | tf_op jit(solution)/shard_map/ppermute | solution.py:30
where the time goes:
time: 352 us; the launch traced here: 351 us
  blocking collectives  210 us (60%)
  waiting for transfers between devices  53.5 us (15%)
  starting transfers between devices  46.9 us (13%)
  other arithmetic  24.4 us (7%)
  between operations  7.8 us (2%)
  local copies, waits for them, and re-layouts  7.6 us (2%)
    psum x3, blocking collectives, squares(): return lax.psum(jnp.sum(field * field), ('gx', 'gy'))  125 us
    psum x2, blocking collectives, per_device(): alpha = norm_now / lax.psum(jnp.sum(direction * image), ('gx', 'gy'))  85.1 us
    ppermute x12, waiting for transfers between devices, padded_2(): lax.ppermute(lax.slice_in_dim(block, block.shape[dim] - width, None, axis...  34.9 us
    ppermute x12, starting transfers between devices, padded_2(): lax.ppermute(lax.slice_in_dim(block, block.shape[dim] - width, None, axis...  29.3 us
    ppermute x12, waiting for transfers between devices, padded_2(): lax.ppermute(lax.slice_in_dim(block, 0, width, axis=dim), axis, backward)  18.6 us
    ppermute x12, starting transfers between devices, padded_2(): lax.ppermute(lax.slice_in_dim(block, 0, width, axis=dim), axis, backward)  17.7 us
  transfers between devices with their start and end apart: 24, of which 20 were waited for; matrix products, arithmetic and copies ran while one was open for 1% of the time, Pallas kernels for 0%

commit v1 on v0

v1 whole, which is shorter than its diff:
```python
import functools

import jax
import jax.numpy as jnp
from jax import lax
from jax.experimental import pallas as pl
from jax.experimental.pallas import tpu as pltpu
from jax.sharding import PartitionSpec as P

MESH = pl.DeviceIdType.MESH
LANES = 128
DIRS = [(dx, dy) for dx in (-1, 0, 1) for dy in (-1, 0, 1) if (dx, dy) != (0, 0)]
SIDES = [(-1, 0), (1, 0), (0, -1), (0, 1)]
TIME_STEP = 0.02
DIAGONAL = 10.0


def kernel(nx, ny, X, Y, S, conc_hbm, order_hbm, disp_hbm, cnew_hbm, onew_hbm,
           nat, xh, ph, v, pot, base, od, oc, gat,
           lsem, osem, a_send, a_recv, v_send, v_recv, p_send, p_recv, g_send, g_recv):
    gx = lax.axis_index("gx")
    gy = lax.axis_index("gy")
    N = nx * ny
    me = gx * ny + gy
    lane = lax.broadcasted_iota(jnp.int32, (S, LANES), 1)
    sub = lax.broadcasted_iota(jnp.int32, (S, LANES), 0)
    last_lane = lane == LANES - 1
    first_lane = lane == 0
    z_end = jnp.logical_and(last_lane, sub == S - 1)
    z_start = jnp.logical_and(first_lane, sub == 0)
    zero = jnp.zeros((S, LANES), jnp.float32)

    loads = [
        pltpu.make_async_copy(conc_hbm, nat.at[0], lsem.at[0]),
        pltpu.make_async_copy(order_hbm, nat.at[pl.ds(1, 3)], lsem.at[1]),
    ]
    for item in loads:
        item.start()

    barrier = pltpu.get_barrier_semaphore()

    def greet(j, carry):
        t = lax.rem(me + j, N)
        pl.semaphore_signal(barrier, inc=1, device_id=(t // ny, lax.rem(t, ny)), device_id_type=MESH)
        return carry

    lax.fori_loop(1, N, greet, 0)
    pl.semaphore_wait(barrier, N - 1)

    def device(dx, dy):
        return (lax.rem(gx + dx + nx, nx), lax.rem(gy + dy + ny, ny))

    def remote(src, dst, send, recv, d):
        return pltpu.make_async_remote_copy(
            src_ref=src, dst_ref=dst, send_sem=send, recv_sem=recv,
            device_id=device(*d), device_id_type=MESH)

    def cell(y):
        return pl.ds(pl.multiple_of(y * S, S), S)

    def own(count, extent, step):
        if step == 0:
            return (pl.ds(1, extent), pl.ds(1, extent))
        return (pl.ds(1, 1), pl.ds(extent + 1, 1)) if step < 0 else (pl.ds(extent, 1), pl.ds(0, 1))

    def rows(part):
        return pl.ds(part.start * S, part.size * S)

    a_copies = []
    for n, (dx, face, side) in enumerate(((-1, 0, 1), (1, X - 1, 0))):
        a_copies.append(remote(conc_hbm.at[face], xh.at[side, 0], a_send.at[2 * n], a_recv.at[2 * n], (dx, 0)))
        a_copies.append(remote(order_hbm.at[:, face], xh.at[side, pl.ds(1, 3)], a_send.at[2 * n + 1],
                               a_recv.at[2 * n + 1], (dx, 0)))
    for item in a_copies:
        item.start()
    for item in loads:
        item.wait()

    def to_cells(read, f, x):
        for y0 in range(0, Y, 8):
            for c in range(S):
                ph[f, x, pl.ds((1 + y0) * S + c, 8, stride=S), :] = read(y0, c)

    def relayout(i, carry):
        f, x = i // X, lax.rem(i, X)
        to_cells(lambda y0, c: nat[f, x, pl.ds(y0, 8), pl.ds(c * LANES, LANES)], f, x + 1)
        return carry

    lax.fori_loop(0, 4 * X, relayout, 0)
    y_copies = []
    for n, dy in enumerate((-1, 1)):
        src, dst = own(ny, Y, dy)
        y_copies.append(remote(ph.at[:, pl.ds(1, X), rows(src)], ph.at[:, pl.ds(1, X), rows(dst)],
                               a_send.at[4 + n], a_recv.at[4 + n], (0, dy)))
    for item in y_copies:
        item.start()
    for item in a_copies:
        item.wait()

    def relayout_x(f, carry):
        for side in range(2):
            to_cells(lambda y0, c: xh[side, f, pl.ds(y0, 8), pl.ds(c * LANES, LANES)], f, side * (X + 1))
        return carry

    lax.fori_loop(0, 4, relayout_x, 0)
    for item in y_copies:
        item.wait()

    def up(a):
        r = pltpu.roll(a, LANES - 1, 1)
        return jnp.where(last_lane, pltpu.roll(r, S - 1, 0), r)

    def down(a):
        r = pltpu.roll(a, 1, 1)
        return jnp.where(first_lane, pltpu.roll(r, 1, 0), r)

    def up0(a):
        return jnp.where(z_end, 0.0, up(a))

    def down0(a):
        return jnp.where(z_start, 0.0, down(a))

    def cells(body, init=0):
        def outer(y, carry):
            for x in range(1, X + 1):
                carry = body(x, y, carry)
            return carry
        return lax.fori_loop(1, Y + 1, outer, init)

    def rhs(x, y, carry):
        def load(f, xx, yy):
            return ph[f, xx, cell(yy), :]

        def eig(a, xx, yy):
            o = load(1 + a, xx, yy)
            return load(0, xx, yy) + o * o
        r0 = -2.5 * (eig(0, x + 1, y) - eig(0, x - 1, y))
        r1 = -2.5 * (eig(1, x, y + 1) - eig(1, x, y - 1))
        e = eig(2, x, y)
        r2 = -2.5 * (up(e) - down(e))
        v[0, 0, x, cell(y), :] = r0
        v[0, 1, x, cell(y), :] = r1
        v[0, 2, x, cell(y), :] = r2
        return carry + (r0 * r0 + r1 * r1 + r2 * r2)

    acc0 = cells(rhs, zero)

    def valid(dx, dy):
        ok = None
        for g, n, d in ((gx, nx, dx), (gy, ny, dy)):
            if d:
                t = g > 0 if d < 0 else g < n - 1
                ok = t if ok is None else jnp.logical_and(ok, t)
        return ok

    def v_copy(k, n):
        dx, dy = DIRS[n]
        sx, tx = own(nx, X, dx)
        sy, ty = own(ny, Y, dy)
        comps = pl.ds(0, 2) if dx and dy else pl.ds(0, 3)
        return remote(v.at[k, comps, sx, rows(sy)], v.at[k, comps, tx, rows(ty)],
                      v_send.at[k, n], v_recv.at[k, n], (dx, dy))

    def v_start(k):
        for n in sorted(range(8), key=lambda n: (DIRS[n][0] == 0, DIRS[n][1] != 0)):
            @pl.when(valid(*DIRS[n]))
            def _():
                v_copy(k, n).start()

    def v_wait(k):
        for n, (dx, dy) in enumerate(DIRS):
            @pl.when(valid(dx, dy))
            def _():
                v_copy(k, n).wait_send()

            @pl.when(valid(-dx, -dy))
            def _():
                v_copy(k, n).wait_recv()

    v_start(0)

    def clear_x(row):
        def body(i, carry):
            for k in range(3):
                for a in range(3):
                    v[k, a, row, cell(i), :] = zero
            return carry
        lax.fori_loop(0, Y + 2, body, 0)

    def clear_y(col, low, high):
        for k in range(3):
            for a in range(3):
                for x in range(low, high):
                    v[k, a, x, cell(col), :] = zero

    for cond, row in ((gx == 0, 0), (gx == nx - 1, X + 1)):
        @pl.when(cond)
        def _(row=row):
            clear_x(row)
    for cond, col in ((gy == 0, 0), (gy == ny - 1, Y + 1)):
        @pl.when(cond)
        def _(col=col):
            clear_y(col, 0, X + 2)

    def laplace(read, x, y):
        c = read(x, y)
        s = read(x + 1, y) + read(x - 1, y) + read(x, y + 1) + read(x, y - 1)
        return s + up(c) + down(c) - 6.0 * c

    def potential(x, y, carry):
        c = ph[0, x, cell(y), :]
        o = [ph[1 + p, x, cell(y), :] for p in range(3)]
        total = o[0] * o[0] + o[1] * o[1] + o[2] * o[2]
        lap = laplace(lambda xx, yy: ph[0, xx, cell(yy), :], x, y)
        pot[x, cell(y), :] = c * c * c - c - 0.5 * total - 0.5 * lap
        return carry

    cells(potential)
    p_copies = []
    for n, (dx, dy) in enumerate(SIDES):
        sx, tx = own(nx, X, dx)
        sy, ty = own(ny, Y, dy)
        p_copies.append(remote(pot.at[sx, rows(sy)], pot.at[tx, rows(ty)], p_send.at[n], p_recv.at[n], (dx, dy)))
    for item in p_copies:
        item.start()

    def stencil(k, x, y):
        def u(a, dx, dy):
            return v[k, a, x + dx, cell(y + dy), :]
        cross = []
        for a in (0, 1):
            cross.append(0.5 * (u(a, 1, 1) - u(a, 1, -1) - u(a, -1, 1) + u(a, -1, -1)))
        xp = [u(a, 1, 0) for a in range(3)]
        xm = [u(a, -1, 0) for a in range(3)]
        yp = [u(a, 0, 1) for a in range(3)]
        ym = [u(a, 0, -1) for a in range(3)]
        c = [u(a, 0, 0) for a in range(3)]
        g = 0.5 * (xp[2] - xm[2])
        h = 0.5 * (yp[2] - ym[2])
        w = 0.5 * ((xp[0] - xm[0]) + (yp[1] - ym[1]))
        i0 = 3.0 * (xp[0] + xm[0]) + (yp[0] + ym[0]) + cross[1] + up0(c[0] + g) + down0(c[0] - g)
        i1 = (xp[1] + xm[1]) + 3.0 * (yp[1] + ym[1]) + cross[0] + up0(c[1] + h) + down0(c[1] - h)
        c3 = 3.0 * c[2]
        i2 = (xp[2] + xm[2]) + (yp[2] + ym[2]) + up0(c3 + w) + down0(c3 - w)
        return c, [i0, i1, i2]

    scale = -1.0 / DIAGONAL

    def first(x, y, carry):
        d01, d11 = carry
        c, image = stencil(0, x, y)
        for a in range(3):
            new = scale * image[a]
            v[1, a, x, cell(y), :] = new
            d01 = d01 + c[a] * new
            d11 = d11 + new * new
        return d01, d11

    v_wait(0)
    acc1 = cells(first, (zero, zero))
    v_start(1)

    def local(x, y, carry):
        c = ph[0, x, cell(y), :]
        o = [ph[1 + p, x, cell(y), :] for p in range(3)]
        q = [item * item for item in o]
        total = q[0] + q[1] + q[2]
        common = total - 1.0 - c
        for p in range(3):
            lap = laplace(lambda xx, yy: ph[1 + p, xx, cell(yy), :], x, y)
            misfit = c + 2.5 * q[p] - 0.5 * total
            trace = 3.0 * c + total
            elastic = 2.5 * (-trace - 2.0 * misfit) + 2.5 * trace
            drive = common * o[p] - 0.5 * lap - 2.0 * o[p] * elastic
            base[p, x - 1, cell(y - 1), :] = o[p] - TIME_STEP * drive
        return carry

    cells(local)

    def second(x, y, carry):
        d12, d22 = carry
        c, image = stencil(1, x, y)
        for a in range(3):
            new = (2.0 * scale) * image[a] - v[0, a, x, cell(y), :]
            v[2, a, x, cell(y), :] = new
            d12 = d12 + c[a] * new
            d22 = d22 + new * new
        return d12, d22

    v_wait(1)
    acc2 = cells(second, (zero, zero))
    v_start(2)

    for item in p_copies:
        item.wait()

    def conc_step(x, y, carry):
        lap = laplace(lambda xx, yy: pot[xx, cell(yy), :], x, y)
        pot_new = ph[0, x, cell(y), :] + TIME_STEP * lap
        oc[x - 1, cell(y - 1), :] = pot_new
        return carry

    cells(conc_step)

    def from_cells(read, f, x):
        for y0 in range(0, Y, 8):
            for c in range(S):
                nat[f, x, pl.ds(y0, 8), pl.ds(c * LANES, LANES)] = read(pl.ds(y0 * S + c, 8, stride=S))

    def conc_out(x, carry):
        from_cells(lambda r: oc[x, r, :], 0, x)
        return carry

    lax.fori_loop(0, X, conc_out, 0)
    c_store = pltpu.make_async_copy(nat.at[0], cnew_hbm, osem.at[0])
    c_store.start()

    def third(x, y, carry):
        c, image = stencil(2, x, y)
        return carry + (c[0] * image[0] + c[1] * image[1] + c[2] * image[2])

    v_wait(2)
    acc3 = scale * cells(third, zero)

    row_lane = lax.broadcasted_iota(jnp.int32, (1, LANES), 1)

    def reduce_all(a):
        return jnp.sum(jnp.sum(a, axis=0, keepdims=True), axis=1, keepdims=True)

    packed = jnp.zeros((1, LANES), jnp.float32)
    for n, item in enumerate((acc0, acc1[0], acc1[1], acc2[0], acc2[1], acc3)):
        packed = jnp.where(row_lane == n, reduce_all(item), packed)
    gat[me] = packed

    def g_copy(j, slot):
        t = lax.rem(me + j, N)
        return pltpu.make_async_remote_copy(
            src_ref=gat.at[slot], dst_ref=gat.at[slot], send_sem=g_send.at[j], recv_sem=g_recv.at[j],
            device_id=(t // ny, lax.rem(t, ny)), device_id_type=MESH)

    def g_start(j, carry):
        g_copy(j, me).start()
        return carry

    def g_wait(j, carry):
        g_copy(j, me).wait_send()
        g_copy(j, lax.rem(me + N - j, N)).wait_recv()
        return carry

    lax.fori_loop(1, N, g_start, 0)
    lax.fori_loop(1, N, g_wait, 0)
    tot = gat[0]
    for j in range(1, N):
        tot = tot + gat[j]
    m0, m1, d11, d12, d22, e = [
        jnp.sum(jnp.where(row_lane == n, tot, 0.0), axis=1, keepdims=True) for n in range(6)]

    g02 = 2.0 * d11 - m0
    G = [[m0, m1, g02], [m1, d11, d12], [g02, d12, d22]]
    h11 = 0.5 * (d12 + m1)
    h12 = 0.5 * (d22 + g02)
    H = [[m1, d11, d12], [d11, h11, h12], [d12, h12, e]]

    def form(mat, a, b):
        out = None
        for i in range(3):
            for j in range(3):
                if a[i] is not None and b[j] is not None:
                    term = a[i] * b[j] * mat[i][j]
                    out = term if out is None else out + term
        return out

    def plus(a, b):
        return b if a is None else (a if b is None else a + b)

    def times(s, a):
        return None if a is None else s * a

    A = [[DIAGONAL * (H[i][j] + G[i][j]) for j in range(3)] for i in range(3)]
    one = jnp.ones((1, 1), jnp.float32)
    xs, rs, ps = [None] * 3, [one, None, None], [one, None, None]
    rr = m0
    for it in range(3):
        alpha = rr / form(A, ps, ps)
        xs = [plus(xs[i], times(alpha, ps[i])) for i in range(3)]
        if it < 2:
            t = list(ps)
            t[1] = plus(t[1], ps[0])
            if ps[1] is not None:
                t[0] = plus(t[0], 0.5 * ps[1])
                t[2] = plus(t[2], 0.5 * ps[1])
            rs = [plus(rs[i], times(-DIAGONAL * alpha, t[i])) for i in range(3)]
            new = form(G, rs, rs)
            ps = [plus(rs[i], times(new / rr, ps[i])) for i in range(3)]
            rr = new
    co = [jnp.broadcast_to(item, (S, LANES)) for item in xs]

    def mix(a, x, y):
        return (co[0] * v[0, a, x, cell(y), :] + co[1] * v[1, a, x, cell(y), :]
                + co[2] * v[2, a, x, cell(y), :])

    def combine(x, y, carry):
        for a in range(3):
            od[a, x, cell(y), :] = mix(a, x, y)
        return carry

    cells(combine)

    def halo_x(y, carry):
        for x in (0, X + 1):
            od[0, x, cell(y), :] = mix(0, x, y)
        return carry

    lax.fori_loop(1, Y + 1, halo_x, 0)
    for x in range(1, X + 1):
        for y in (0, Y + 1):
            od[1, x, cell(y), :] = mix(1, x, y)

    c_store.wait()

    def disp_out(i, carry):
        a, x = i // X, lax.rem(i, X)
        for y0 in range(0, Y, 8):
            for c in range(S):
                nat[a, x, pl.ds(y0, 8), pl.ds(c * LANES, LANES)] = od[
                    a, x + 1, pl.ds((1 + y0) * S + c, 8, stride=S), :]
        return carry

    lax.fori_loop(0, 3 * X, disp_out, 0)
    d_store = pltpu.make_async_copy(nat.at[pl.ds(0, 3)], disp_hbm, osem.at[1])
    d_store.start()

    def final(x, y, carry):
        d2 = od[2, x, cell(y), :]
        strain = [
            0.5 * (od[0, x + 1, cell(y), :] - od[0, x - 1, cell(y), :]),
            0.5 * (od[1, x, cell(y + 1), :] - od[1, x, cell(y - 1), :]),
            0.5 * (up0(d2) - down0(d2)),
        ]
        trace = strain[0] + strain[1] + strain[2]
        for p in range(3):
            elastic = 2.5 * (trace + 2.0 * strain[p]) - 2.5 * trace
            base[p, x - 1, cell(y - 1), :] = (
                base[p, x - 1, cell(y - 1), :] + (2.0 * TIME_STEP) * ph[1 + p, x, cell(y), :] * elastic)
        return carry

    cells(final)
    d_store.wait()

    def order_out(i, carry):
        a, x = i // X, lax.rem(i, X)
        from_cells(lambda r: base[a, x, r, :], a, x)
        return carry

    lax.fori_loop(0, 3 * X, order_out, 0)
    o_store = pltpu.make_async_copy(nat.at[pl.ds(0, 3)], onew_hbm, osem.at[2])
    o_store.start()
    o_store.wait()


def solution(mesh):
    nx, ny = mesh.shape["gx"], mesh.shape["gy"]

    def step(conc, order):
        X, Y, Z = conc.shape
        S = Z // LANES
        f32 = jnp.float32
        N = nx * ny
        dma = pltpu.SemaphoreType.DMA
        anyspace = pl.BlockSpec(memory_space=pl.ANY)
        return pl.pallas_call(
            functools.partial(kernel, nx, ny, X, Y, S),
            out_shape=(jax.ShapeDtypeStruct(order.shape, f32), jax.ShapeDtypeStruct(conc.shape, f32),
                       jax.ShapeDtypeStruct(order.shape, f32)),
            in_specs=[anyspace] * 2,
            out_specs=[anyspace] * 3,
            scratch_shapes=[
                pltpu.VMEM((4, X, Y, Z), f32),
                pltpu.VMEM((2, 4, Y, Z), f32),
                pltpu.VMEM((4, X + 2, (Y + 2) * S, LANES), f32),
                pltpu.VMEM((3, 3, X + 2, (Y + 2) * S, LANES), f32),
                pltpu.VMEM((X + 2, (Y + 2) * S, LANES), f32),
                pltpu.VMEM((3, X, Y * S, LANES), f32),
                pltpu.VMEM((3, X + 2, (Y + 2) * S, LANES), f32),
                pltpu.VMEM((X, Y * S, LANES), f32),
                pltpu.VMEM((N, 1, LANES), f32),
                dma((2,)), dma((3,)), dma((6,)), dma((6,)),
                dma((3, 8)), dma((3, 8)), dma((4,)), dma((4,)), dma((N,)), dma((N,)),
            ],
            compiler_params=pltpu.CompilerParams(
                collective_id=0, has_side_effects=True, vmem_limit_bytes=48 << 20),
        )(conc, order)

    return jax.shard_map(
        step,
        mesh=mesh,
        in_specs=(P("gx", "gy", None), P(None, "gx", "gy", None)),
        out_specs=(P(None, "gx", "gy", None), P("gx", "gy", None), P(None, "gx", "gy", None)),
        check_vma=False,
    )
```

time: 352 us -> 73.1 us (0.21)
  blocking collectives: 210 us -> 0 us
  Pallas kernels: 0 us -> 67.7 us
  waiting for transfers between devices: 53.5 us -> 0 us
  starting transfers between devices: 46.9 us -> 0 us
  other arithmetic: 24.4 us -> 0 us
  between operations: 7.8 us -> 0.65 us
    psum x5 -> x0, blocking collectives: 210 us -> none  [the longest x3 125 us: squares(): return lax.psum(jnp.sum(field * field), ('gx', 'gy'))]
    pallas_call x0 -> x1, Pallas kernels: none -> 67.7 us  [step(): pl.pallas_call(functools.partial(kernel, nx, ny, X, Y, S), out_shape=(jax...]
    ppermute x24 -> x0, waiting for transfers between devices: 53.5 us -> none  [the longest x12 34.9 us: padded_2(): lax.ppermute(lax.slice_in_dim(block, block.shape[dim] - width, None, axis...]
    ppermute x24 -> x0, starting transfers between devices: 46.9 us -> none  [the longest x12 29.3 us: padded_2(): lax.ppermute(lax.slice_in_dim(block, block.shape[dim] - width, None, axis...]
    concatenate x12 -> x0, other arithmetic: 6.13 us -> none  [padded_2(): block = jnp.concatenate([low, block, high], axis=dim)]
    sub x11 -> x0, other arithmetic: 5.93 us -> none  [the longest x9 4.61 us: stencil(): -SHEAR_MODULUS * laplace - (LAME_LAMBDA + SHEAR_MODULUS) * graddiv]
    add x7 -> x0, other arithmetic: 4.45 us -> none  [the longest x2 1.45 us: per_device(): direction = residual + norm_next / norm_now * direction]
    reduce_sum x5 -> x0, other arithmetic: 4.24 us -> none  [the longest x3 2.6 us: per_device(): alpha = norm_now / lax.psum(jnp.sum(direction * image), ('gx', 'gy'))]
  transfers between devices with their start and end apart: 24 -> 0, of which waited for: 20 -> 0; matrix products, arithmetic and copies ran while one was open for 1% -> 0% of each run, Pallas kernels for 0% -> 0%
where the time goes in v1:
time: 73.1 us; the launch traced here: 72.9 us
  Pallas kernels  67.7 us (93%)
  local copies, waits for them, and re-layouts  4.54 us (6%)
    pallas_call x1, Pallas kernels, step(): pl.pallas_call(functools.partial(kernel, nx, ny, X, Y, S), out_shape=(jax...  67.7 us
    unnamed x7, local copies, waits for them, and re-layouts  4.54 us

profile of v1, /device:TPU:0, one launch (start us, length us, event | category | flops | bytes accessed | tf_op | source)
XLA Modules:
  0.0 72.9 jit_solution(10964211231290303840)
XLA Ops:
  0.6 0.0 copy-start
  0.6 1.1 %copy-done = f32[3,4,16,1024]{3,2,1,0:T(8,128)S(1)} copy-done((f32[3,4,16,1024]{3,2,1,0:T(8,128)S(1)}, f32[3,4,16,1024]{3,2,1,0:T(8,128)}, u32[]{:S(2)}) %copy-start) | copy-done | bytes 786456
  1.8 0.0 copy-start.1
  1.8 0.9 %copy-done.1 = f32[4,16,1024]{2,1,0:T(8,128)S(1)} copy-done((f32[4,16,1024]{2,1,0:T(8,128)S(1)}, f32[4,16,1024]{2,1,0:T(8,128)}, u32[]{:S(2)}) %copy-start.1) | copy-done | bytes 262168
  2.7 67.7 %shard_map.49 = (f32[3,4,16,1024]{3,2,1,0:T(8,128)S(1)}, f32[4,16,1024]{2,1,0:T(8,128)S(1)}, f32[3,4,16,1024]{3,2,1,0:T(8,128)S(1)}) custom-call(f32[4,16,1024]{2,1,0:T(8,128)S(1)} %copy-done.1, f32[3,4,16,1024]{3,2,1,0:T(8,128)S(1)} %copy-done), custom_call_target="tpu_custom_call" | custom-call | tf_op jit(solution)/shard_map/pallas_call | solution.py:471
  70.5 0.9 %copy.8 = f32[3,4,16,1024]{3,2,1,0:T(8,128)} copy(f32[3,4,16,1024]{3,2,1,0:T(8,128)S(1)} %get-tuple-element.6) | data formatting | bytes 1572864
  71.3 0.7 copy.9
  72.1 0.9 %copy.10 = f32[3,4,16,1024]{3,2,1,0:T(8,128)} copy(f32[3,4,16,1024]{3,2,1,0:T(8,128)S(1)} %get-tuple-element.8) | data formatting | bytes 1572864
Async XLA Ops:
  0.6 1.1 %copy-start = (f32[3,4,16,1024]{3,2,1,0:T(8,128)S(1)}, f32[3,4,16,1024]{3,2,1,0:T(8,128)}, u32[]{:S(2)}) copy-start(f32[3,4,16,1024]{3,2,1,0:T(8,128)} %order_hbm.1) | copy-start | bytes 2359300
  1.8 0.9 %copy-start.1 = (f32[4,16,1024]{2,1,0:T(8,128)S(1)}, f32[4,16,1024]{2,1,0:T(8,128)}, u32[]{:S(2)}) copy-start(f32[4,16,1024]{2,1,0:T(8,128)} %conc_hbm.1) | copy-start | bytes 786436

commit v2 on v1

--- a/solution.py
+++ b/solution.py
@@ -10,14 +10,13 @@
 MESH = pl.DeviceIdType.MESH
 LANES = 128
 DIRS = [(dx, dy) for dx in (-1, 0, 1) for dy in (-1, 0, 1) if (dx, dy) != (0, 0)]
-SIDES = [(-1, 0), (1, 0), (0, -1), (0, 1)]
 TIME_STEP = 0.02
 DIAGONAL = 10.0
 
 
-def kernel(nx, ny, X, Y, S, conc_hbm, order_hbm, disp_hbm, cnew_hbm, onew_hbm,
+def kernel(nx, ny, X, Y, S, conc_hbm, order_hbm, disp_out, cnew_out, onew_out,
            nat, xh, ph, v, pot, base, od, oc, gat,
-           lsem, osem, a_send, a_recv, v_send, v_recv, p_send, p_recv, g_send, g_recv):
+           lsem, a_send, a_recv, v_send, v_recv, g_send, g_recv):
     gx = lax.axis_index("gx")
     gy = lax.axis_index("gy")
     N = nx * ny
@@ -45,7 +44,6 @@
         return carry
 
     lax.fori_loop(1, N, greet, 0)
-    pl.semaphore_wait(barrier, N - 1)
 
     def device(dx, dy):
         return (lax.rem(gx + dx + nx, nx), lax.rem(gy + dy + ny, ny))
@@ -66,45 +64,66 @@
     def rows(part):
         return pl.ds(part.start * S, part.size * S)
 
-    a_copies = []
-    for n, (dx, face, side) in enumerate(((-1, 0, 1), (1, X - 1, 0))):
-        a_copies.append(remote(conc_hbm.at[face], xh.at[side, 0], a_send.at[2 * n], a_recv.at[2 * n], (dx, 0)))
-        a_copies.append(remote(order_hbm.at[:, face], xh.at[side, pl.ds(1, 3)], a_send.at[2 * n + 1],
-                               a_recv.at[2 * n + 1], (dx, 0)))
-    for item in a_copies:
-        item.start()
-    for item in loads:
-        item.wait()
-
     def to_cells(read, f, x):
         for y0 in range(0, Y, 8):
             for c in range(S):
-                ph[f, x, pl.ds((1 + y0) * S + c, 8, stride=S), :] = read(y0, c)
+                ph[f, x, pl.ds((2 + y0) * S + c, 8, stride=S), :] = read(y0, c)
 
     def relayout(i, carry):
         f, x = i // X, lax.rem(i, X)
-        to_cells(lambda y0, c: nat[f, x, pl.ds(y0, 8), pl.ds(c * LANES, LANES)], f, x + 1)
-        return carry
-
+        to_cells(lambda y0, c: nat[f, x, pl.ds(y0, 8), pl.ds(c * LANES, LANES)], f, x + 2)
+        return carry
+
+    for item in loads:
+        item.wait()
     lax.fori_loop(0, 4 * X, relayout, 0)
-    y_copies = []
-    for n, dy in enumerate((-1, 1)):
-        src, dst = own(ny, Y, dy)
-        y_copies.append(remote(ph.at[:, pl.ds(1, X), rows(src)], ph.at[:, pl.ds(1, X), rows(dst)],
-                               a_send.at[4 + n], a_recv.at[4 + n], (0, dy)))
-    for item in y_copies:
-        item.start()
-    for item in a_copies:
+    pl.semaphore_wait(barrier, N - 1)
+
+    copies = []
+
+    def send(src, dst, d):
+        n = len(copies)
+        copies.append(remote(src, dst, a_send.at[n], a_recv.at[n], d))
+        copies[-1].start()
+
+    def two(extent, step):
+        if step < 0:
+            return (2, extent + 2), (3, extent + 3), (2, extent + 2)
+        return (extent + 1, 1), (extent, 0), (extent, 0)
+
+    for dx, near, far, side in ((-1, 0, 1, 1), (1, X - 1, X - 2, 0)):
+        send(conc_hbm.at[near], xh.at[side, 0], (dx, 0))
+        send(order_hbm.at[:, near], xh.at[side, pl.ds(2, 3)], (dx, 0))
+    for dx in (-1, 1):
+        xn, xf, _ = two(X, dx)
+        for dy in (-1, 1):
+            yn, _, yb = two(Y, dy)
+            send(ph.at[pl.ds(0, 3), xn[0], pl.ds(yb[0] * S, 2 * S)],
+                 ph.at[pl.ds(0, 3), xn[1], pl.ds(yb[1] * S, 2 * S)], (dx, dy))
+            send(ph.at[pl.ds(0, 2), xf[0], pl.ds(yn[0] * S, S)],
+                 ph.at[pl.ds(0, 2), xf[1], pl.ds(yn[1] * S, S)], (dx, dy))
+    for dx, near, far, side in ((-1, 0, 1, 1), (1, X - 1, X - 2, 0)):
+        send(conc_hbm.at[far], xh.at[side, 1], (dx, 0))
+        send(order_hbm.at[0, far], xh.at[side, 5], (dx, 0))
+    for dy in (-1, 1):
+        yn, _, yb = two(Y, dy)
+        send(ph.at[pl.ds(0, 3), pl.ds(2, X), pl.ds(yb[0] * S, 2 * S)],
+             ph.at[pl.ds(0, 3), pl.ds(2, X), pl.ds(yb[1] * S, 2 * S)], (0, dy))
+        send(ph.at[3, pl.ds(2, X), pl.ds(yn[0] * S, S)],
+             ph.at[3, pl.ds(2, X), pl.ds(yn[1] * S, S)], (0, dy))
+    for item in copies:
         item.wait()
 
-    def relayout_x(f, carry):
-        for side in range(2):
-            to_cells(lambda y0, c: xh[side, f, pl.ds(y0, 8), pl.ds(c * LANES, LANES)], f, side * (X + 1))
-        return carry
-
-    lax.fori_loop(0, 4, relayout_x, 0)
-    for item in y_copies:
-        item.wait()
+    def relayout_x(i, carry):
+        for slot, f, far in ((0, 0, 0), (1, 0, 1), (2, 1, 0), (3, 2, 0), (4, 3, 0), (5, 1, 1)):
+            row = (1 - far) + i * (X + 1 + 2 * far)
+            to_cells(lambda y0, c: xh[i, slot, pl.ds(y0, 8), pl.ds(c * LANES, LANES)], f, row)
+        return carry
+
+    lax.fori_loop(0, 2, relayout_x, 0)
+
+    def phase(f, x, y):
+        return ph[f, x + 1, cell(y + 1), :]
 
     def up(a):
         r = pltpu.roll(a, LANES - 1, 1)
@@ -120,30 +139,55 @@
     def down0(a):
         return jnp.where(z_start, 0.0, down(a))
 
-    def cells(body, init=0):
+    def cells(body, init=0, over=range(1, X + 1)):
         def outer(y, carry):
-            for x in range(1, X + 1):
+            for x in over:
                 carry = body(x, y, carry)
             return carry
         return lax.fori_loop(1, Y + 1, outer, init)
 
+    edge_rows = sorted({1, X})
+    inner_rows = list(range(2, X))
+
+    def eig(a, x, y):
+        o = phase(1 + a, x, y)
+        return phase(0, x, y) + o * o
+
+    def rhs_at(x, y, comps):
+        out = []
+        for a in range(comps):
+            if a == 0:
+                r = -2.5 * (eig(0, x + 1, y) - eig(0, x - 1, y))
+            elif a == 1:
+                r = -2.5 * (eig(1, x, y + 1) - eig(1, x, y - 1))
+            else:
+                e = eig(2, x, y)
+                r = -2.5 * (up(e) - down(e))
+            v[0, a, x, cell(y), :] = r
+            out.append(r)
+        return out
+
     def rhs(x, y, carry):
-        def load(f, xx, yy):
-            return ph[f, xx, cell(yy), :]
-
-        def eig(a, xx, yy):
-            o = load(1 + a, xx, yy)
-            return load(0, xx, yy) + o * o
-        r0 = -2.5 * (eig(0, x + 1, y) - eig(0, x - 1, y))
-        r1 = -2.5 * (eig(1, x, y + 1) - eig(1, x, y - 1))
-        e = eig(2, x, y)
-        r2 = -2.5 * (up(e) - down(e))
-        v[0, 0, x, cell(y), :] = r0
-        v[0, 1, x, cell(y), :] = r1
-        v[0, 2, x, cell(y), :] = r2
+        r0, r1, r2 = rhs_at(x, y, 3)
         return carry + (r0 * r0 + r1 * r1 + r2 * r2)
 
+    def rhs_halo(x, y, carry):
+        rhs_at(x, y, 3)
+        return carry
+
+    def y_halo(body):
+        def outer(x, carry):
+            for y in (0, Y + 1):
+                body(x, y, 0)
+            return carry
+        lax.fori_loop(1, X + 1, outer, 0)
+
     acc0 = cells(rhs, zero)
+    cells(rhs_halo, over=(0, X + 1))
+    y_halo(rhs_halo)
+    for x in (0, X + 1):
+        for y in (0, Y + 1):
+            rhs_at(x, y, 2)
 
     def valid(dx, dy):
         ok = None
@@ -157,18 +201,24 @@
         dx, dy = DIRS[n]
         sx, tx = own(nx, X, dx)
         sy, ty = own(ny, Y, dy)
-        comps = pl.ds(0, 2) if dx and dy else pl.ds(0, 3)
+        comps = pl.ds(0, 2) if dx and dy else pl.ds(0, 1) if k == 2 and dx > 0 else pl.ds(0, 3)
         return remote(v.at[k, comps, sx, rows(sy)], v.at[k, comps, tx, rows(ty)],
-                      v_send.at[k, n], v_recv.at[k, n], (dx, dy))
-
-    def v_start(k):
-        for n in sorted(range(8), key=lambda n: (DIRS[n][0] == 0, DIRS[n][1] != 0)):
-            @pl.when(valid(*DIRS[n]))
-            def _():
-                v_copy(k, n).start()
+                      v_send.at[k - 1, n], v_recv.at[k - 1, n], (dx, dy))
+
+    def v_dirs(k):
+        return [n for n in range(8) if not (k == 2 and DIRS[n][0] > 0 and DIRS[n][1])]
+
+    def v_start(k, along_x):
+        for n in sorted(v_dirs(k), key=lambda n: DIRS[n][1] != 0):
+            if (DIRS[n][0] != 0) == along_x:
+                @pl.when(valid(*DIRS[n]))
+                def _(n=n):
+                    v_copy(k, n).start()
 
     def v_wait(k):
-        for n, (dx, dy) in enumerate(DIRS):
+        for n in v_dirs(k):
+            dx, dy = DIRS[n]
+
             @pl.when(valid(dx, dy))
             def _():
                 v_copy(k, n).wait_send()
@@ -176,8 +226,6 @@
             @pl.when(valid(-dx, -dy))
             def _():
                 v_copy(k, n).wait_recv()
-
-    v_start(0)
 
     def clear_x(row):
         def body(i, carry):
@@ -208,25 +256,19 @@
         return s + up(c) + down(c) - 6.0 * c
 
     def potential(x, y, carry):
-        c = ph[0, x, cell(y), :]
-        o = [ph[1 + p, x, cell(y), :] for p in range(3)]
+        c = phase(0, x, y)
+        o = [phase(1 + p, x, y) for p in range(3)]
         total = o[0] * o[0] + o[1] * o[1] + o[2] * o[2]
-        lap = laplace(lambda xx, yy: ph[0, xx, cell(yy), :], x, y)
+        lap = laplace(functools.partial(phase, 0), x, y)
         pot[x, cell(y), :] = c * c * c - c - 0.5 * total - 0.5 * lap
         return carry
 
-    cells(potential)
-    p_copies = []
-    for n, (dx, dy) in enumerate(SIDES):
-        sx, tx = own(nx, X, dx)
-        sy, ty = own(ny, Y, dy)
-        p_copies.append(remote(pot.at[sx, rows(sy)], pot.at[tx, rows(ty)], p_send.at[n], p_recv.at[n], (dx, dy)))
-    for item in p_copies:
-        item.start()
-
-    def stencil(k, x, y):
+    def stencil(k, x, y, one_sided=False):
         def u(a, dx, dy):
-            return v[k, a, x + dx, cell(y + dy), :]
+            if one_sided and x + dx == 0:
+                return zero
+            value = v[k, a, x + dx, cell(y + dy), :]
+            return 2.0 * value if one_sided and x + dx == X + 1 else value
         cross = []
         for a in (0, 1):
             cross.append(0.5 * (u(a, 1, 1) - u(a, 1, -1) - u(a, -1, 1) + u(a, -1, -1)))
@@ -256,21 +298,24 @@
             d11 = d11 + new * new
         return d01, d11
 
-    v_wait(0)
-    acc1 = cells(first, (zero, zero))
-    v_start(1)
+    acc1 = cells(first, (zero, zero), edge_rows)
+    v_start(1, True)
+    acc1 = cells(first, acc1, inner_rows)
+    v_start(1, False)
+    cells(potential)
+    cells(potential, over=(0, X + 1))
+    y_halo(potential)
 
     def local(x, y, carry):
-        c = ph[0, x, cell(y), :]
-        o = [ph[1 + p, x, cell(y), :] for p in range(3)]
+        c = phase(0, x, y)
+        o = [phase(1 + p, x, y) for p in range(3)]
         q = [item * item for item in o]
         total = q[0] + q[1] + q[2]
         common = total - 1.0 - c
         for p in range(3):
-            lap = laplace(lambda xx, yy: ph[1 + p, xx, cell(yy), :], x, y)
+            lap = laplace(functools.partial(phase, 1 + p), x, y)
             misfit = c + 2.5 * q[p] - 0.5 * total
-            trace = 3.0 * c + total
-            elastic = 2.5 * (-trace - 2.0 * misfit) + 2.5 * trace
+            elastic = -5.0 * misfit
             drive = common * o[p] - 0.5 * lap - 2.0 * o[p] * elastic
             base[p, x - 1, cell(y - 1), :] = o[p] - TIME_STEP * drive
         return carry
@@ -288,35 +333,33 @@
         return d12, d22
 
     v_wait(1)
-    acc2 = cells(second, (zero, zero))
-    v_start(2)
-
-    for item in p_copies:
-        item.wait()
+    acc2 = cells(second, (zero, zero), edge_rows)
+    v_start(2, True)
+    acc2 = cells(second, acc2, inner_rows)
+    v_start(2, False)
 
     def conc_step(x, y, carry):
         lap = laplace(lambda xx, yy: pot[xx, cell(yy), :], x, y)
-        pot_new = ph[0, x, cell(y), :] + TIME_STEP * lap
-        oc[x - 1, cell(y - 1), :] = pot_new
+        oc[x - 1, cell(y - 1), :] = phase(0, x, y) + TIME_STEP * lap
         return carry
 
     cells(conc_step)
 
-    def from_cells(read, f, x):
+    def from_cells(write, read, first):
         for y0 in range(0, Y, 8):
             for c in range(S):
-                nat[f, x, pl.ds(y0, 8), pl.ds(c * LANES, LANES)] = read(pl.ds(y0 * S + c, 8, stride=S))
+                write(pl.ds(y0, 8), pl.ds(c * LANES, LANES), read(pl.ds((first + y0) * S + c, 8, stride=S)))
 
     def conc_out(x, carry):
-        from_cells(lambda r: oc[x, r, :], 0, x)
+        def write(r, l, value):
+            cnew_out[x, r, l] = value
+        from_cells(write, lambda r: oc[x, r, :], 0)
         return carry
 
     lax.fori_loop(0, X, conc_out, 0)
-    c_store = pltpu.make_async_copy(nat.at[0], cnew_hbm, osem.at[0])
-    c_store.start()
 
     def third(x, y, carry):
-        c, image = stencil(2, x, y)
+        c, image = stencil(2, x, y, True)
         return carry + (c[0] * image[0] + c[1] * image[1] + c[2] * image[2])
 
     v_wait(2)
@@ -416,19 +459,15 @@
         for y in (0, Y + 1):
             od[1, x, cell(y), :] = mix(1, x, y)
 
-    c_store.wait()
-
-    def disp_out(i, carry):
+    def disp_store(i, carry):
         a, x = i // X, lax.rem(i, X)
-        for y0 in range(0, Y, 8):
-            for c in range(S):
-                nat[a, x, pl.ds(y0, 8), pl.ds(c * LANES, LANES)] = od[
-                    a, x + 1, pl.ds((1 + y0) * S + c, 8, stride=S), :]
-        return carry
-
-    lax.fori_loop(0, 3 * X, disp_out, 0)
-    d_store = pltpu.make_async_copy(nat.at[pl.ds(0, 3)], disp_hbm, osem.at[1])
-    d_store.start()
+
+        def write(r, l, value):
+            disp_out[a, x, r, l] = value
+        from_cells(write, lambda r: od[a, x + 1, r, :], 1)
+        return carry
+
+    lax.fori_loop(0, 3 * X, disp_store, 0)
 
     def final(x, y, carry):
         d2 = od[2, x, cell(y), :]
@@ -437,25 +476,23 @@
             0.5 * (od[1, x, cell(y + 1), :] - od[1, x, cell(y - 1), :]),
             0.5 * (up0(d2) - down0(d2)),
         ]
-        trace = strain[0] + strain[1] + strain[2]
         for p in range(3):
-            elastic = 2.5 * (trace + 2.0 * strain[p]) - 2.5 * trace
             base[p, x - 1, cell(y - 1), :] = (
-                base[p, x - 1, cell(y - 1), :] + (2.0 * TIME_STEP) * ph[1 + p, x, cell(y), :] * elastic)
+                base[p, x - 1, cell(y - 1), :]
+                + (10.0 * TIME_STEP) * phase(1 + p, x, y) * strain[p])
         return carry
 
     cells(final)
-    d_store.wait()
-
-    def order_out(i, carry):
+
+    def order_store(i, carry):
         a, x = i // X, lax.rem(i, X)
-        from_cells(lambda r: base[a, x, r, :], a, x)
-        return carry
-
-    lax.fori_loop(0, 3 * X, order_out, 0)
-    o_store = pltpu.make_async_copy(nat.at[pl.ds(0, 3)], onew_hbm, osem.at[2])
-    o_store.start()
-    o_store.wait()
+
+        def write(r, l, value):
+            onew_out[a, x, r, l] = value
+        from_cells(write, lambda r: base[a, x, r, :], 0)
+        return carry
+
+    lax.fori_loop(0, 3 * X, order_store, 0)
 
 
 def solution(mesh):
@@ -467,25 +504,23 @@
         f32 = jnp.float32
         N = nx * ny
         dma = pltpu.SemaphoreType.DMA
-        anyspace = pl.BlockSpec(memory_space=pl.ANY)
         return pl.pallas_call(
             functools.partial(kernel, nx, ny, X, Y, S),
             out_shape=(jax.ShapeDtypeStruct(order.shape, f32), jax.ShapeDtypeStruct(conc.shape, f32),
                        jax.ShapeDtypeStruct(order.shape, f32)),
-            in_specs=[anyspace] * 2,
-            out_specs=[anyspace] * 3,
+            in_specs=[pl.BlockSpec(memory_space=pltpu.HBM)] * 2,
+            out_specs=[pl.BlockSpec(memory_space=pltpu.VMEM)] * 3,
             scratch_shapes=[
                 pltpu.VMEM((4, X, Y, Z), f32),
-                pltpu.VMEM((2, 4, Y, Z), f32),
-                pltpu.VMEM((4, X + 2, (Y + 2) * S, LANES), f32),
+                pltpu.VMEM((2, 6, Y, Z), f32),
+                pltpu.VMEM((4, X + 4, (Y + 4) * S, LANES), f32),
                 pltpu.VMEM((3, 3, X + 2, (Y + 2) * S, LANES), f32),
                 pltpu.VMEM((X + 2, (Y + 2) * S, LANES), f32),
                 pltpu.VMEM((3, X, Y * S, LANES), f32),
                 pltpu.VMEM((3, X + 2, (Y + 2) * S, LANES), f32),
                 pltpu.VMEM((X, Y * S, LANES), f32),
                 pltpu.VMEM((N, 1, LANES), f32),
-                dma((2,)), dma((3,)), dma((6,)), dma((6,)),
-                dma((3, 8)), dma((3, 8)), dma((4,)), dma((4,)), dma((N,)), dma((N,)),
+                dma((2,)), dma((20,)), dma((20,)), dma((2, 8)), dma((2, 8)), dma((N,)), dma((N,)),
             ],
             compiler_params=pltpu.CompilerParams(
                 collective_id=0, has_side_effects=True, vmem_limit_bytes=48 << 20),

time: 73.1 us -> 67.1 us (0.918)
  Pallas kernels: 67.7 us -> 61.7 us
    pallas_call x1, Pallas kernels: 67.7 us -> 61.7 us  [step(): pl.pallas_call(functools.partial(kernel, nx, ny, X, Y, S), out_shape=(jax...]
where the time goes in v2:
time: 67.1 us; the launch traced here: 66.9 us
  Pallas kernels  61.7 us (92%)
  local copies, waits for them, and re-layouts  4.54 us (7%)
    pallas_call x1, Pallas kernels, step(): pl.pallas_call(functools.partial(kernel, nx, ny, X, Y, S), out_shape=(jax...  61.7 us
    unnamed x7, local copies, waits for them, and re-layouts  4.54 us

profile of v2, /device:TPU:0, one launch (start us, length us, event | category | flops | bytes accessed | tf_op | source)
XLA Modules:
  0.0 66.9 jit_solution(14153033245598287361)
XLA Ops:
  0.6 0.0 copy-start
  0.6 1.1 %copy-done = f32[3,4,16,1024]{3,2,1,0:T(8,128)S(1)} copy-done((f32[3,4,16,1024]{3,2,1,0:T(8,128)S(1)}, f32[3,4,16,1024]{3,2,1,0:T(8,128)}, u32[]{:S(2)}) %copy-start) | copy-done | bytes 786456
  1.8 0.0 copy-start.1
  1.8 0.9 %copy-done.1 = f32[4,16,1024]{2,1,0:T(8,128)S(1)} copy-done((f32[4,16,1024]{2,1,0:T(8,128)S(1)}, f32[4,16,1024]{2,1,0:T(8,128)}, u32[]{:S(2)}) %copy-start.1) | copy-done | bytes 262168
  2.7 61.7 %shard_map.49 = (f32[3,4,16,1024]{3,2,1,0:T(8,128)S(1)}, f32[4,16,1024]{2,1,0:T(8,128)S(1)}, f32[3,4,16,1024]{3,2,1,0:T(8,128)S(1)}) custom-call(f32[4,16,1024]{2,1,0:T(8,128)S(1)} %copy-done.1, f32[3,4,16,1024]{3,2,1,0:T(8,128)S(1)} %copy-done), custom_call_target="tpu_custom_call" | custom-call | tf_op jit(solution)/shard_map/pallas_call | solution.py:507
  64.4 0.9 %copy.8 = f32[3,4,16,1024]{3,2,1,0:T(8,128)} copy(f32[3,4,16,1024]{3,2,1,0:T(8,128)S(1)} %get-tuple-element.6) | data formatting | bytes 1572864
  65.3 0.7 %copy.9 = f32[4,16,1024]{2,1,0:T(8,128)} copy(f32[4,16,1024]{2,1,0:T(8,128)S(1)} %get-tuple-element.7) | data formatting | bytes 524288
  66.0 0.9 %copy.10 = f32[3,4,16,1024]{3,2,1,0:T(8,128)} copy(f32[3,4,16,1024]{3,2,1,0:T(8,128)S(1)} %get-tuple-element.8) | data formatting | bytes 1572864
Async XLA Ops:
  0.6 1.1 %copy-start = (f32[3,4,16,1024]{3,2,1,0:T(8,128)S(1)}, f32[3,4,16,1024]{3,2,1,0:T(8,128)}, u32[]{:S(2)}) copy-start(f32[3,4,16,1024]{3,2,1,0:T(8,128)} %order_hbm.1) | copy-start | bytes 2359300
  1.8 0.9 %copy-start.1 = (f32[4,16,1024]{2,1,0:T(8,128)S(1)}, f32[4,16,1024]{2,1,0:T(8,128)}, u32[]{:S(2)}) copy-start(f32[4,16,1024]{2,1,0:T(8,128)} %conc_hbm.1) | copy-start | bytes 786436

commit v3 on v2

--- a/solution.py
+++ b/solution.py
@@ -15,7 +15,7 @@
 
 
 def kernel(nx, ny, X, Y, S, conc_hbm, order_hbm, disp_out, cnew_out, onew_out,
-           nat, xh, ph, v, pot, base, od, oc, gat,
+           nat, far_e, xh, ph, v, pot, base, od, oc, gat,
            lsem, a_send, a_recv, v_send, v_recv, g_send, g_recv):
     gx = lax.axis_index("gx")
     gy = lax.axis_index("gy")
@@ -69,14 +69,23 @@
             for c in range(S):
                 ph[f, x, pl.ds((2 + y0) * S + c, 8, stride=S), :] = read(y0, c)
 
-    def relayout(i, carry):
-        f, x = i // X, lax.rem(i, X)
-        to_cells(lambda y0, c: nat[f, x, pl.ds(y0, 8), pl.ds(c * LANES, LANES)], f, x + 2)
+    def spread(read, x):
+        for y0 in range(0, Y, 8):
+            for c in range(S):
+                o = [read(1 + p, y0, c) for p in range(3)]
+                conc = read(0, y0, c)
+                for f, value in enumerate(o + [conc, conc + o[0] * o[0], conc + o[1] * o[1]]):
+                    ph[f, x, pl.ds((2 + y0) * S + c, 8, stride=S), :] = value
+
+    def relayout(x, carry):
+        spread(lambda f, y0, c: nat[f, x, pl.ds(y0, 8), pl.ds(c * LANES, LANES)], x + 2)
         return carry
 
     for item in loads:
         item.wait()
-    lax.fori_loop(0, 4 * X, relayout, 0)
+    lax.fori_loop(0, X, relayout, 0)
+    for side, far in ((1, 1), (0, X - 2)):
+        far_e[side] = nat[0, far] + nat[1, far] * nat[1, far]
     pl.semaphore_wait(barrier, N - 1)
 
     copies = []
@@ -91,39 +100,25 @@
             return (2, extent + 2), (3, extent + 3), (2, extent + 2)
         return (extent + 1, 1), (extent, 0), (extent, 0)
 
-    for dx, near, far, side in ((-1, 0, 1, 1), (1, X - 1, X - 2, 0)):
+    for dx, near, side in ((-1, 0, 1), (1, X - 1, 0)):
         send(conc_hbm.at[near], xh.at[side, 0], (dx, 0))
-        send(order_hbm.at[:, near], xh.at[side, pl.ds(2, 3)], (dx, 0))
+        send(order_hbm.at[:, near], xh.at[side, pl.ds(1, 3)], (dx, 0))
+        send(far_e.at[side], xh.at[side, 4], (dx, 0))
     for dx in (-1, 1):
         xn, xf, _ = two(X, dx)
         for dy in (-1, 1):
-            yn, _, yb = two(Y, dy)
-            send(ph.at[pl.ds(0, 3), xn[0], pl.ds(yb[0] * S, 2 * S)],
-                 ph.at[pl.ds(0, 3), xn[1], pl.ds(yb[1] * S, 2 * S)], (dx, dy))
-            send(ph.at[pl.ds(0, 2), xf[0], pl.ds(yn[0] * S, S)],
-                 ph.at[pl.ds(0, 2), xf[1], pl.ds(yn[1] * S, S)], (dx, dy))
-    for dx, near, far, side in ((-1, 0, 1, 1), (1, X - 1, X - 2, 0)):
-        send(conc_hbm.at[far], xh.at[side, 1], (dx, 0))
-        send(order_hbm.at[0, far], xh.at[side, 5], (dx, 0))
+            yn, yf, _ = two(Y, dy)
+            for fields, xx, yy in ((pl.ds(3, 3), xn, yn), (pl.ds(4, 1), xf, yn), (pl.ds(5, 1), xn, yf)):
+                send(ph.at[fields, xx[0], pl.ds(yy[0] * S, S)],
+                     ph.at[fields, xx[1], pl.ds(yy[1] * S, S)], (dx, dy))
     for dy in (-1, 1):
-        yn, _, yb = two(Y, dy)
-        send(ph.at[pl.ds(0, 3), pl.ds(2, X), pl.ds(yb[0] * S, 2 * S)],
-             ph.at[pl.ds(0, 3), pl.ds(2, X), pl.ds(yb[1] * S, 2 * S)], (0, dy))
-        send(ph.at[3, pl.ds(2, X), pl.ds(yn[0] * S, S)],
-             ph.at[3, pl.ds(2, X), pl.ds(yn[1] * S, S)], (0, dy))
-    for item in copies:
-        item.wait()
-
-    def relayout_x(i, carry):
-        for slot, f, far in ((0, 0, 0), (1, 0, 1), (2, 1, 0), (3, 2, 0), (4, 3, 0), (5, 1, 1)):
-            row = (1 - far) + i * (X + 1 + 2 * far)
-            to_cells(lambda y0, c: xh[i, slot, pl.ds(y0, 8), pl.ds(c * LANES, LANES)], f, row)
-        return carry
-
-    lax.fori_loop(0, 2, relayout_x, 0)
-
-    def phase(f, x, y):
-        return ph[f, x + 1, cell(y + 1), :]
+        yn, yf, _ = two(Y, dy)
+        for fields, yy in ((pl.ds(0, 6), yn), (pl.ds(3, 3), yf)):
+            send(ph.at[fields, pl.ds(2, X), pl.ds(yy[0] * S, S)],
+                 ph.at[fields, pl.ds(2, X), pl.ds(yy[1] * S, S)], (0, dy))
+    urgent = len(copies)
+    for dx, far, side in ((-1, 1, 1), (1, X - 2, 0)):
+        send(conc_hbm.at[far], xh.at[side, 5], (dx, 0))
 
     def up(a):
         r = pltpu.roll(a, LANES - 1, 1)
@@ -139,55 +134,64 @@
     def down0(a):
         return jnp.where(z_start, 0.0, down(a))
 
-    def cells(body, init=0, over=range(1, X + 1)):
+    def cells(body, init=0, over=range(1, X + 1), low=1, high=Y + 1, unroll=2):
         def outer(y, carry):
             for x in over:
                 carry = body(x, y, carry)
             return carry
-        return lax.fori_loop(1, Y + 1, outer, init)
+        return lax.fori_loop(low, high, outer, init, unroll=unroll)
 
     edge_rows = sorted({1, X})
     inner_rows = list(range(2, X))
 
-    def eig(a, x, y):
-        o = phase(1 + a, x, y)
-        return phase(0, x, y) + o * o
+    def phase(f, x, y):
+        return ph[f, x + 1, cell(y + 1), :]
 
     def rhs_at(x, y, comps):
         out = []
         for a in range(comps):
             if a == 0:
-                r = -2.5 * (eig(0, x + 1, y) - eig(0, x - 1, y))
+                r = -2.5 * (phase(4, x + 1, y) - phase(4, x - 1, y))
             elif a == 1:
-                r = -2.5 * (eig(1, x, y + 1) - eig(1, x, y - 1))
+                r = -2.5 * (phase(5, x, y + 1) - phase(5, x, y - 1))
             else:
-                e = eig(2, x, y)
+                o = phase(2, x, y)
+                e = phase(3, x, y) + o * o
                 r = -2.5 * (up(e) - down(e))
             v[0, a, x, cell(y), :] = r
             out.append(r)
         return out
 
     def rhs(x, y, carry):
-        r0, r1, r2 = rhs_at(x, y, 3)
-        return carry + (r0 * r0 + r1 * r1 + r2 * r2)
-
-    def rhs_halo(x, y, carry):
-        rhs_at(x, y, 3)
-        return carry
+        out = rhs_at(x, y, 3)
+        if 1 <= x <= X:
+            carry = carry + (out[0] * out[0] + out[1] * out[1] + out[2] * out[2])
+        return carry
+
+    acc0 = cells(rhs, zero, inner_rows, 2, Y)
+    for item in copies[:urgent]:
+        item.wait()
+
+    def relayout_x(i, carry):
+        spread(lambda f, y0, c: xh[i, f, pl.ds(y0, 8), pl.ds(c * LANES, LANES)], 1 + i * (X + 1))
+        to_cells(lambda y0, c: xh[i, 4, pl.ds(y0, 8), pl.ds(c * LANES, LANES)], 4, i * (X + 3))
+        return carry
+
+    lax.fori_loop(0, 2, relayout_x, 0)
+    acc0 = cells(rhs, acc0, [0] + edge_rows + [X + 1])
+    for x in inner_rows:
+        for y in (1, Y):
+            acc0 = rhs(x, y, acc0)
+    for x in range(0, X + 2):
+        for y in (0, Y + 1):
+            rhs_at(x, y, 3 if 1 <= x <= X else 2)
 
     def y_halo(body):
         def outer(x, carry):
             for y in (0, Y + 1):
                 body(x, y, 0)
             return carry
-        lax.fori_loop(1, X + 1, outer, 0)
-
-    acc0 = cells(rhs, zero)
-    cells(rhs_halo, over=(0, X + 1))
-    y_halo(rhs_halo)
-    for x in (0, X + 1):
-        for y in (0, Y + 1):
-            rhs_at(x, y, 2)
+        lax.fori_loop(1, X + 1, outer, 0, unroll=2)
 
     def valid(dx, dy):
         ok = None
@@ -256,10 +260,10 @@
         return s + up(c) + down(c) - 6.0 * c
 
     def potential(x, y, carry):
-        c = phase(0, x, y)
-        o = [phase(1 + p, x, y) for p in range(3)]
+        c = phase(3, x, y)
+        o = [phase(p, x, y) for p in range(3)]
         total = o[0] * o[0] + o[1] * o[1] + o[2] * o[2]
-        lap = laplace(functools.partial(phase, 0), x, y)
+        lap = laplace(functools.partial(phase, 3), x, y)
         pot[x, cell(y), :] = c * c * c - c - 0.5 * total - 0.5 * lap
         return carry
 
@@ -302,18 +306,21 @@
     v_start(1, True)
     acc1 = cells(first, acc1, inner_rows)
     v_start(1, False)
-    cells(potential)
-    cells(potential, over=(0, X + 1))
+    for item in copies[urgent:]:
+        item.wait()
+    for side in range(2):
+        to_cells(lambda y0, c: xh[side, 5, pl.ds(y0, 8), pl.ds(c * LANES, LANES)], 3, side * (X + 3))
+    cells(potential, over=range(0, X + 2))
     y_halo(potential)
 
     def local(x, y, carry):
-        c = phase(0, x, y)
-        o = [phase(1 + p, x, y) for p in range(3)]
+        c = phase(3, x, y)
+        o = [phase(p, x, y) for p in range(3)]
         q = [item * item for item in o]
         total = q[0] + q[1] + q[2]
         common = total - 1.0 - c
         for p in range(3):
-            lap = laplace(functools.partial(phase, 1 + p), x, y)
+            lap = laplace(functools.partial(phase, p), x, y)
             misfit = c + 2.5 * q[p] - 0.5 * total
             elastic = -5.0 * misfit
             drive = common * o[p] - 0.5 * lap - 2.0 * o[p] * elastic
@@ -340,7 +347,7 @@
 
     def conc_step(x, y, carry):
         lap = laplace(lambda xx, yy: pot[xx, cell(yy), :], x, y)
-        oc[x - 1, cell(y - 1), :] = phase(0, x, y) + TIME_STEP * lap
+        oc[x - 1, cell(y - 1), :] = phase(3, x, y) + TIME_STEP * lap
         return carry
 
     cells(conc_step)
@@ -479,7 +486,7 @@
         for p in range(3):
             base[p, x - 1, cell(y - 1), :] = (
                 base[p, x - 1, cell(y - 1), :]
-                + (10.0 * TIME_STEP) * phase(1 + p, x, y) * strain[p])
+                + (10.0 * TIME_STEP) * phase(p, x, y) * strain[p])
         return carry
 
     cells(final)
@@ -512,15 +519,16 @@
             out_specs=[pl.BlockSpec(memory_space=pltpu.VMEM)] * 3,
             scratch_shapes=[
                 pltpu.VMEM((4, X, Y, Z), f32),
+                pltpu.VMEM((2, Y, Z), f32),
                 pltpu.VMEM((2, 6, Y, Z), f32),
-                pltpu.VMEM((4, X + 4, (Y + 4) * S, LANES), f32),
+                pltpu.VMEM((6, X + 4, (Y + 4) * S, LANES), f32),
                 pltpu.VMEM((3, 3, X + 2, (Y + 2) * S, LANES), f32),
                 pltpu.VMEM((X + 2, (Y + 2) * S, LANES), f32),
                 pltpu.VMEM((3, X, Y * S, LANES), f32),
                 pltpu.VMEM((3, X + 2, (Y + 2) * S, LANES), f32),
                 pltpu.VMEM((X, Y * S, LANES), f32),
                 pltpu.VMEM((N, 1, LANES), f32),
-                dma((2,)), dma((20,)), dma((20,)), dma((2, 8)), dma((2, 8)), dma((N,)), dma((N,)),
+                dma((2,)), dma((24,)), dma((24,)), dma((2, 8)), dma((2, 8)), dma((N,)), dma((N,)),
             ],
             compiler_params=pltpu.CompilerParams(
                 collective_id=0, has_side_effects=True, vmem_limit_bytes=48 << 20),

time: 67.1 us -> 60.2 us (0.90)
  Pallas kernels: 61.7 us -> 54.9 us
    pallas_call x1, Pallas kernels: 61.7 us -> 54.9 us  [step(): pl.pallas_call(functools.partial(kernel, nx, ny, X, Y, S), out_shape=(jax...]
where the time goes in v3:
time: 60.2 us; the launch traced here: 60.1 us
  Pallas kernels  54.9 us (91%)
  local copies, waits for them, and re-layouts  4.54 us (8%)
  between operations  0.65 us (1%)
    pallas_call x1, Pallas kernels, step(): pl.pallas_call(functools.partial(kernel, nx, ny, X, Y, S), out_shape=(jax...  54.9 us
    unnamed x7, local copies, waits for them, and re-layouts  4.54 us

profile of v3, /device:TPU:0, one launch (start us, length us, event | category | flops | bytes accessed | tf_op | source)
XLA Modules:
  0.0 60.1 jit_solution(12726631198351391010)
XLA Ops:
  0.6 0.0 copy-start
  0.6 1.1 %copy-done = f32[3,4,16,1024]{3,2,1,0:T(8,128)S(1)} copy-done((f32[3,4,16,1024]{3,2,1,0:T(8,128)S(1)}, f32[3,4,16,1024]{3,2,1,0:T(8,128)}, u32[]{:S(2)}) %copy-start) | copy-done | bytes 786456
  1.8 0.0 copy-start.1
  1.8 0.9 %copy-done.1 = f32[4,16,1024]{2,1,0:T(8,128)S(1)} copy-done((f32[4,16,1024]{2,1,0:T(8,128)S(1)}, f32[4,16,1024]{2,1,0:T(8,128)}, u32[]{:S(2)}) %copy-start.1) | copy-done | bytes 262168
  2.7 54.9 %shard_map.49 = (f32[3,4,16,1024]{3,2,1,0:T(8,128)S(1)}, f32[4,16,1024]{2,1,0:T(8,128)S(1)}, f32[3,4,16,1024]{3,2,1,0:T(8,128)S(1)}) custom-call(f32[4,16,1024]{2,1,0:T(8,128)S(1)} %copy-done.1, f32[3,4,16,1024]{3,2,1,0:T(8,128)S(1)} %copy-done), custom_call_target="tpu_custom_call" | custom-call | tf_op jit(solution)/shard_map/pallas_call | solution.py:514
  57.6 0.9 %copy.8 = f32[3,4,16,1024]{3,2,1,0:T(8,128)} copy(f32[3,4,16,1024]{3,2,1,0:T(8,128)S(1)} %get-tuple-element.6) | data formatting | bytes 1572864
  58.5 0.7 %copy.9 = f32[4,16,1024]{2,1,0:T(8,128)} copy(f32[4,16,1024]{2,1,0:T(8,128)S(1)} %get-tuple-element.7) | data formatting | bytes 524288
  59.2 0.9 %copy.10 = f32[3,4,16,1024]{3,2,1,0:T(8,128)} copy(f32[3,4,16,1024]{3,2,1,0:T(8,128)S(1)} %get-tuple-element.8) | data formatting | bytes 1572864
Async XLA Ops:
  0.6 1.1 %copy-start = (f32[3,4,16,1024]{3,2,1,0:T(8,128)S(1)}, f32[3,4,16,1024]{3,2,1,0:T(8,128)}, u32[]{:S(2)}) copy-start(f32[3,4,16,1024]{3,2,1,0:T(8,128)} %order_hbm.1) | copy-start | bytes 2359300
  1.8 0.9 %copy-start.1 = (f32[4,16,1024]{2,1,0:T(8,128)S(1)}, f32[4,16,1024]{2,1,0:T(8,128)}, u32[]{:S(2)}) copy-start(f32[4,16,1024]{2,1,0:T(8,128)} %conc_hbm.1) | copy-start | bytes 786436
